TPU v7x, 1024 devices: a whole 4x8x16 slice. The times are simulated.
1024 devices in a mesh: ctx: 8 (over y), exp: 64 (over z, x), rep: 2 (over core).
Axes of the slice: x: 4, y: 8, z: 16, core: 2. Of those that a mesh axis runs over, the one named last changes fastest.
Arguments:
- tokens: bfloat16 [16384, 7168], P(('rep', 'exp'), 'ctx'), parts along dimension 0, may hold values from -6 to 6
- routes: int32 [16384, 2], P(('rep', 'exp')), parts along dimension 0, may hold values from 0 to 63, all different within a row; in each aligned block of 128 rows (0 to 127, 128 to 255, ...) at most 5 rows name the same one
- event_weights: float32 [16384, 2], P(('rep', 'exp')), parts along dimension 0, may hold values from 0.25 to 2
- cotangent: bfloat16 [8192, 7168], P('exp', 'ctx'), may hold values from -0.59765625 to 0.59765625
- w_gate: bfloat16 [64, 7168, 1024], P('exp', 'ctx'), may hold values from -0.0625 to 0.0625
- w_up: bfloat16 [64, 7168, 1024], P('exp', 'ctx'), may hold values from -0.0625 to 0.0625
- w_down: bfloat16 [64, 1024, 7168], P('exp', None, 'ctx'), may hold values from -0.1875 to 0.1875
Outputs:
- mixed: bfloat16 [16384, 7168], P(('rep', 'exp'), 'ctx'), parts along dimension 0
- token_grad: bfloat16 [16384, 7168], P(('rep', 'exp'), 'ctx'), parts along dimension 0
- weight_grad: float32 [16384, 2], P(('rep', 'exp')), parts along dimension 0
There are 2 independent parts, one for each index of `rep`. A program takes and returns all parts, laid end to end along the dimension named above; an argument that names none is the same for every part. Nothing has to cross between parts.
Inputs may be any that keep to these rules, and one draw needn't show every extreme that they name: `routes`: each token names 2 different experts. Among the 128 tokens of one index of exp (aligned blocks of 128 rows) no expert is named more than 5 times, a bound that some block reaches; every expert is named somewhere.
All inputs are finite; a program needn't handle non-finite values.
Results may differ from a plain program's by a relative error of at most 0.03.
Values may be sent and summed in bfloat16 or wider, within the bound.
No kernel may reach another device: no remote copies, remote signals or barrier semaphores. Data moves between devices by JAX's collectives and lax.ppermute only.
A program may use at most 32 MiB of HBM per device.

v0:
```python
import jax
import jax.numpy as jnp
from jax import lax
from jax.sharding import PartitionSpec as P


def activate(gate_pre, up_pre, back_pre):
    squash = jax.nn.sigmoid(gate_pre)
    hidden_act = (gate_pre * squash * up_pre).astype(jnp.bfloat16)
    grad_gate = (back_pre * up_pre * squash * (1.0 + gate_pre * (1.0 - squash))).astype(
        jnp.bfloat16
    )
    grad_up = (back_pre * gate_pre * squash).astype(jnp.bfloat16)
    return (hidden_act, grad_gate, grad_up)


def shards(tokens, routes, event_weights, cotangent, w_gate, w_up, w_down):
    owners = lax.axis_size("exp")
    owned, columns, hidden = w_gate.shape
    experts = owned * owners
    rows_here, fanout = routes.shape
    capacity = max(2, 5 * rows_here * fanout // (4 * experts))
    slot_count = owners * capacity
    routes_flat = routes.reshape(-1)
    onehot = (routes_flat[:, None] == jnp.arange(experts, dtype=jnp.int32)[None, :]).astype(
        jnp.int32
    )
    places = jnp.sum((jnp.cumsum(onehot, axis=0) - onehot) * onehot, axis=1)
    targets = routes_flat * capacity + places
    token_rows = jnp.repeat(tokens, fanout, axis=0)
    cot_rows = (
        event_weights.reshape(-1, 1) * jnp.repeat(cotangent.astype(jnp.float32), fanout, axis=0)
    ).astype(jnp.bfloat16)
    send_tokens = jnp.zeros((experts * capacity, columns), jnp.bfloat16).at[targets].set(token_rows)
    send_cots = jnp.zeros((experts * capacity, columns), jnp.bfloat16).at[targets].set(cot_rows)
    send_tokens = send_tokens.reshape(owners, owned * capacity, columns)
    send_cots = send_cots.reshape(owners, owned * capacity, columns)
    recv_tokens, recv_cots = (
        lax.all_to_all(send_tokens, "exp", split_axis=0, concat_axis=0, tiled=True),
        lax.all_to_all(send_cots, "exp", split_axis=0, concat_axis=0, tiled=True),
    )

    def arrange(buffer):
        return (
            buffer.reshape(owners, owned, capacity, columns)
            .transpose(1, 0, 2, 3)
            .reshape(owned, slot_count, columns)
        )

    expert_in = arrange(recv_tokens)
    expert_cot = arrange(recv_cots)
    partials = (
        jnp.einsum("jsd,jdf->fjs", expert_in, w_gate, preferred_element_type=jnp.float32),
        jnp.einsum("jsd,jdf->fjs", expert_in, w_up, preferred_element_type=jnp.float32),
        jnp.einsum("jsd,jfd->fjs", expert_cot, w_down, preferred_element_type=jnp.float32),
    )
    gate_pre, up_pre, back_pre = (
        lax.psum(partials[0].astype(jnp.bfloat16), "ctx").astype(jnp.float32),
        lax.psum(partials[1].astype(jnp.bfloat16), "ctx").astype(jnp.float32),
        lax.psum(partials[2].astype(jnp.bfloat16), "ctx").astype(jnp.float32),
    )
    hidden_act, grad_gate, grad_up = activate(gate_pre, up_pre, back_pre)
    expert_out = jnp.einsum(
        "fjs,jfd->jsd", hidden_act, w_down, preferred_element_type=jnp.float32
    ).astype(jnp.bfloat16)
    event_grad = (
        jnp.einsum("fjs,jdf->jsd", grad_gate, w_gate, preferred_element_type=jnp.float32)
        + jnp.einsum("fjs,jdf->jsd", grad_up, w_up, preferred_element_type=jnp.float32)
    ).astype(jnp.bfloat16)

    def restore(buffer):
        return (
            buffer.reshape(owned, owners, capacity, columns)
            .transpose(1, 0, 2, 3)
            .reshape(owners, owned * capacity, columns)
        )

    back_out, back_grad = (
        lax.all_to_all(restore(expert_out), "exp", split_axis=0, concat_axis=0, tiled=True),
        lax.all_to_all(restore(event_grad), "exp", split_axis=0, concat_axis=0, tiled=True),
    )
    out_rows = (
        back_out.reshape(experts * capacity, columns)[targets]
        .reshape(rows_here, fanout, columns)
        .astype(jnp.float32)
    )
    grad_rows = (
        back_grad.reshape(experts * capacity, columns)[targets]
        .reshape(rows_here, fanout, columns)
        .astype(jnp.float32)
    )
    mixed = jnp.sum(event_weights[:, :, None] * out_rows, axis=1).astype(jnp.bfloat16)
    token_grad = jnp.sum(grad_rows, axis=1).astype(jnp.bfloat16)
    weight_part = jnp.einsum("td,tkd->tk", cotangent.astype(jnp.float32), out_rows)
    weight_grad = lax.psum(weight_part, "ctx")
    return (mixed, token_grad, weight_grad)


def solution(mesh):
    in_specs = (
        P(("rep", "exp"), "ctx"),
        P(("rep", "exp"), None),
        P(("rep", "exp"), None),
        P("exp", "ctx"),
        P("exp", "ctx", None),
        P("exp", "ctx", None),
        P("exp", None, "ctx"),
    )
    out_specs = (P(("rep", "exp"), "ctx"), P(("rep", "exp"), "ctx"), P(("rep", "exp"), None))
    return jax.shard_map(shards, mesh=mesh, in_specs=in_specs, out_specs=out_specs, check_vma=False)
```

profile of v0, /device:TPU:4, one launch (start us, length us, event | category | flops | bytes accessed | tf_op | source)
XLA Modules:
  0.0 384.3 jit_solution(5254923358020531812)
XLA Ops:
  10.2 1.2 broadcast_in_dim.4
  11.7 1.8 scatter_custom_fusion
  13.5 1.2 reshape.129
  14.7 22.6 %all-to-all-start = ((bf16[64,5,896]{2,1,0:T(8,128)(2,1)}), bf16[64,5,896]{2,1,0:T(8,128)(2,1)}, u32[]{:S(2)}, u32[]{:S(2)}) async-start(bf16[64,5,896]{2,1,0:T(8,128)(2,1)} %reshape.129), calls=%async_computation | async-start | bytes 1835008 | tf_op jit(solution)/shard_map/all_to_all | solution.py:39
  37.5 1.2 broadcast_in_dim.5
  38.7 1.8 reshape.137
  40.5 1.9 scatter_custom_fusion.1
  42.4 1.2 reshape.138
  43.5 43.2 %all-to-all-done = bf16[64,5,896]{2,1,0:T(8,128)(2,1)} async-done(((bf16[64,5,896]{2,1,0:T(8,128)(2,1)}), bf16[64,5,896]{2,1,0:T(8,128)(2,1)}, u32[]{:S(2)}, u32[]{:S(2)}) %all-to-all-start) | async-done | bytes 573472 | tf_op jit(solution)/shard_map/all_to_all | solution.py:39
  86.8 5.9 %all-to-all-start.2 = ((bf16[64,5,896]{2,1,0:T(8,128)(2,1)}), bf16[64,5,896]{2,1,0:T(8,128)(2,1)S(1)}, u32[]{:S(2)}, u32[]{:S(2)}) async-start(bf16[64,5,896]{2,1,0:T(8,128)(2,1)} %reshape.138), calls=%async_computation.2 | async-start | bytes 1835008 | tf_op jit(solution)/shard_map/all_to_all | solution.py:40
  92.9 1.4 reshape.130
  94.4 1.7 fusion.43
  96.1 1.7 fusion.46
  97.8 44.0 %all-to-all-done.2 = bf16[64,5,896]{2,1,0:T(8,128)(2,1)S(1)} async-done(((bf16[64,5,896]{2,1,0:T(8,128)(2,1)}), bf16[64,5,896]{2,1,0:T(8,128)(2,1)S(1)}, u32[]{:S(2)}, u32[]{:S(2)}) %all-to-all-start.2) | async-done | bytes 573472 | tf_op jit(solution)/shard_map/all_to_all | solution.py:40
  142.0 3.2 fusion.40
  145.2 89.4 %all-reduce.3.cloned.1.call-done = (bf16[1024,1,320]{0,2,1:T(8,128)(2,1)}, bf16[1024,1,320]{0,2,1:T(8,128)(2,1)}, bf16[1024,1,320]{0,2,1:T(8,128)(2,1)}) async-done(((bf16[1024,1,320]{0,2,1:T(8,128)(2,1)}, bf16[1024,1,320]{0,2,1:T(8,128)(2,1)}, bf16[1024,1,320]{0,2,1:T(8,128)(2,1)}), (bf16[1024,1,320]{0,2,1:T(8,128)(2,1)}, bf16[1024,1,320]{0,2,1:T(8,128)(2,1)}, ...) | async-done | bytes 1966096 | tf_op jit(solution)/shard_map/psum | solution.py:59
  234.7 2.4 fusion.4
  237.1 1.2 fusion.24
  238.3 1.2 reshape_transpose_reshape.9
  239.5 16.4 %all-to-all-start.3 = ((bf16[64,5,896]{2,1,0:T(8,128)(2,1)}), bf16[64,5,896]{2,1,0:T(8,128)(2,1)S(1)}, u32[]{:S(2)}, u32[]{:S(2)}) async-start(bf16[64,5,896]{2,1,0:T(8,128)(2,1)} %reshape_transpose_reshape.9), calls=%async_computation.3 | async-start | bytes 1835008 | tf_op jit(solution)/shard_map/all_to_all | solution.py:80
  256.0 2.8 fusion.27
  258.8 1.1 reshape_transpose_reshape.8
  260.0 41.5 %all-to-all-done.3 = bf16[64,5,896]{2,1,0:T(8,128)(2,1)S(1)} async-done(((bf16[64,5,896]{2,1,0:T(8,128)(2,1)}), bf16[64,5,896]{2,1,0:T(8,128)(2,1)S(1)}, u32[]{:S(2)}, u32[]{:S(2)}) %all-to-all-start.3) | async-done | bytes 573472 | tf_op jit(solution)/shard_map/all_to_all | solution.py:80
  301.4 6.1 %all-to-all-start.1 = ((bf16[64,5,896]{2,1,0:T(8,128)(2,1)}), bf16[64,5,896]{2,1,0:T(8,128)(2,1)}, u32[]{:S(2)}, u32[]{:S(2)}) async-start(bf16[64,5,896]{2,1,0:T(8,128)(2,1)} %reshape_transpose_reshape.8), calls=%async_computation.1 | async-start | bytes 1835008 | tf_op jit(solution)/shard_map/all_to_all | solution.py:79
  307.8 1.2 gather_fusion.1
  309.2 1.9 reduce_sum.35
  311.1 43.5 %all-to-all-done.1 = bf16[64,5,896]{2,1,0:T(8,128)(2,1)} async-done(((bf16[64,5,896]{2,1,0:T(8,128)(2,1)}), bf16[64,5,896]{2,1,0:T(8,128)(2,1)}, u32[]{:S(2)}, u32[]{:S(2)}) %all-to-all-start.1) | async-done | bytes 573472 | tf_op jit(solution)/shard_map/all_to_all | solution.py:79
  354.6 1.4 reshape.135
  356.0 1.2 gather_fusion
  357.4 1.9 multiply_reduce_fusion
  359.3 1.2 fusion.57
  360.6 16.8 %psum.31 = f32[128,2]{0,1:T(2,128)} all-reduce(f32[128,2]{0,1:T(2,128)S(1)} %bitcast.83), channel_id=1, replica_groups=mesh['ctx'=8,'exp'=64,'rep'=2] {'ctx'}, use_global_device_ids=true, to_apply=%region_10.11 | all-reduce | flops 256 | bytes 2048 | tf_op jit(solution)/shard_map/psum | solution.py:95
  (42 shorter events, 4.7 us)
Async XLA Ops:
  7.2 87.2 %copy-start = (bf16[1,896,1024]{2,1,0:T(8,128)(2,1)S(1)}, bf16[1,896,1024]{2,1,0:T(8,128)(2,1)}, u32[]{:S(2)}) copy-start(bf16[1,896,1024]{2,1,0:T(8,128)(2,1)} %param.12) | copy-start | bytes 5505028
  13.5 23.8 %copy-start.3 = (f32[128,2]{0,1:T(2,128)S(1)}, f32[128,2]{0,1:T(2,128)}, u32[]{:S(2)}) copy-start(f32[128,2]{0,1:T(2,128)} %param.9) | copy-start | bytes 3076
  14.7 22.9 %copy-start.1 = (bf16[128,896]{1,0:T(8,128)(2,1)S(1)}, bf16[128,896]{1,0:T(8,128)(2,1)}, u32[]{:S(2)}) copy-start(bf16[128,896]{1,0:T(8,128)(2,1)} %param.10) | copy-start | bytes 688132
  14.7 72.1 %all-to-all-start = ((bf16[64,5,896]{2,1,0:T(8,128)(2,1)}), bf16[64,5,896]{2,1,0:T(8,128)(2,1)}, u32[]{:S(2)}, u32[]{:S(2)}) async-start(bf16[64,5,896]{2,1,0:T(8,128)(2,1)} %reshape.129), calls=%async_computation | async-start | bytes 1835008 | tf_op jit(solution)/shard_map/all_to_all | solution.py:39
  86.8 55.0 %all-to-all-start.2 = ((bf16[64,5,896]{2,1,0:T(8,128)(2,1)}), bf16[64,5,896]{2,1,0:T(8,128)(2,1)S(1)}, u32[]{:S(2)}, u32[]{:S(2)}) async-start(bf16[64,5,896]{2,1,0:T(8,128)(2,1)} %reshape.138), calls=%async_computation.2 | async-start | bytes 1835008 | tf_op jit(solution)/shard_map/all_to_all | solution.py:40
  92.7 142.0 %all-reduce.3.cloned.1.call-start = ((), (), s32[]{:S(2)}) async-start(), calls=%async_computation.4 | async-start | bytes 3932160 | tf_op jit(solution)/shard_map/psum | solution.py:59
  94.4 1.7 copy-start.4
  234.7 2.4 copy-start.5
  234.7 2.4 copy-start.6
  234.7 2.4 copy-start.7
  234.7 2.4 copy-start.8
  239.5 61.9 %all-to-all-start.3 = ((bf16[64,5,896]{2,1,0:T(8,128)(2,1)}), bf16[64,5,896]{2,1,0:T(8,128)(2,1)S(1)}, u32[]{:S(2)}, u32[]{:S(2)}) async-start(bf16[64,5,896]{2,1,0:T(8,128)(2,1)} %reshape_transpose_reshape.9), calls=%async_computation.3 | async-start | bytes 1835008 | tf_op jit(solution)/shard_map/all_to_all | solution.py:80
  301.4 53.1 %all-to-all-start.1 = ((bf16[64,5,896]{2,1,0:T(8,128)(2,1)}), bf16[64,5,896]{2,1,0:T(8,128)(2,1)}, u32[]{:S(2)}, u32[]{:S(2)}) async-start(bf16[64,5,896]{2,1,0:T(8,128)(2,1)} %reshape_transpose_reshape.8), calls=%async_computation.1 | async-start | bytes 1835008 | tf_op jit(solution)/shard_map/all_to_all | solution.py:79
  357.2 2.1 copy-start.2
Sparse Core Ops, SparseCore 0:
  145.4 89.2 all-reduce.2
where the time goes:
time: 385 us; the launch traced here: 384 us
  waiting for transfers between devices  262 us (68%)
  starting transfers between devices  51.3 us (13%)
  local copies, waits for them, and re-layouts  18.8 us (5%)
  blocking collectives  16.8 us (4%)
  between operations  14.3 us (4%)
  matrix products  14.2 us (4%)
  other arithmetic  7.16 us (2%)
    psum x1, waiting for transfers between devices, shards(): lax.psum(partials[1].astype(jnp.bfloat16), 'ctx').astype(jnp.float32)  89.4 us
    all_to_all x1, waiting for transfers between devices, shards(): lax.all_to_all(send_cots, 'exp', split_axis=0, concat_axis=0, tiled=True)  44 us
    all_to_all x1, waiting for transfers between devices, shards(): lax.all_to_all(restore(expert_out), 'exp', split_axis=0, concat_axis=0, t...  43.5 us
    all_to_all x1, waiting for transfers between devices, shards(): lax.all_to_all(send_tokens, 'exp', split_axis=0, concat_axis=0, tiled=True)  43.2 us
    all_to_all x1, waiting for transfers between devices, shards(): lax.all_to_all(restore(event_grad), 'exp', split_axis=0, concat_axis=0, t...  41.5 us
    all_to_all x1, starting transfers between devices, shards(): lax.all_to_all(send_tokens, 'exp', split_axis=0, concat_axis=0, tiled=True)  22.6 us
    psum x1, blocking collectives, shards(): weight_grad = lax.psum(weight_part, 'ctx')  16.8 us
    all_to_all x1, starting transfers between devices, shards(): lax.all_to_all(restore(event_grad), 'exp', split_axis=0, concat_axis=0, t...  16.4 us
  transfers between devices with their start and end apart: 5, of which 5 were waited for; matrix products, arithmetic and copies ran while one was open for 5% of the time, Pallas kernels for 0%

commit v1 on v0

v1 whole, which is shorter than its diff:
```python
import jax
import jax.numpy as jnp
from jax import lax
from jax.sharding import PartitionSpec as P

LANES = 128
F32 = jnp.float32
BF16 = jnp.bfloat16


def matmul(a, b):
    return jnp.dot(a, b, preferred_element_type=F32)


def shards(tokens, routes, event_weights, cotangent, w_gate, w_up, w_down):
    owners = lax.axis_size("exp")
    parts = lax.axis_size("ctx")
    rows, fanout = routes.shape
    _, columns, hidden = w_gate.shape
    capacity = max(2, 5 * rows * fanout // (4 * owners))
    slots = owners * capacity
    piece = hidden // parts
    tiles = capacity * columns // LANES

    flat = routes.reshape(-1)
    named = (flat[:, None] == jnp.arange(owners, dtype=jnp.int32)[None, :]).astype(BF16)
    events = rows * fanout
    earlier = (
        jnp.arange(events)[:, None] > jnp.arange(events)[None, :]
    ).astype(BF16)
    before = matmul(earlier, named)
    places = jnp.sum(before * named.astype(F32), axis=1).astype(jnp.int32)
    targets = (flat * capacity + places).reshape(rows, fanout)
    slot_ids = jnp.arange(slots, dtype=jnp.int32)
    picks = [slot_ids[:, None] == targets[:, k][None, :] for k in range(fanout)]
    pick_any = sum(p.astype(BF16) for p in picks)
    slot_weights = sum(
        jnp.sum(jnp.where(p, event_weights[:, k][None, :], 0.0), axis=1)
        for k, p in enumerate(picks)
    )

    def send(buffer):
        return lax.all_to_all(buffer, "exp", split_axis=0, concat_axis=0, tiled=True)

    send_tokens = matmul(pick_any, tokens).astype(BF16).reshape(owners, tiles, LANES)
    expert_in = send(send_tokens).reshape(slots, columns)
    send_cots = (
        (slot_weights[:, None] * matmul(pick_any, cotangent)).astype(BF16).reshape(owners, tiles, LANES)
    )
    expert_in, send_cots = lax.optimization_barrier((expert_in, send_cots))
    expert_cot = send(send_cots).reshape(slots, columns)

    gate_w = w_gate[0].reshape(columns, parts, piece)
    up_w = w_up[0].reshape(columns, parts, piece)
    down_w = w_down[0].reshape(parts, piece, columns)

    def scatter(value):
        return lax.psum_scatter(value, "ctx", scatter_dimension=0, tiled=False)

    gate_up = jnp.concatenate(
        [
            jnp.einsum("sd,dyj->ysj", expert_in, gate_w, preferred_element_type=F32).astype(BF16),
            jnp.einsum("sd,dyj->ysj", expert_in, up_w, preferred_element_type=F32).astype(BF16),
        ],
        axis=1,
    )
    gate_up = scatter(gate_up).astype(F32)
    gate_pre, up_pre = gate_up[:slots], gate_up[slots:]
    back = jnp.einsum("sd,yjd->ysj", expert_cot, down_w, preferred_element_type=F32).astype(BF16)

    squash = jax.nn.sigmoid(gate_pre)
    hidden_act = (gate_pre * squash * up_pre).astype(BF16)
    hidden_all = lax.all_gather(hidden_act, "ctx", axis=0, tiled=False)
    expert_out = jnp.einsum("ysj,yjd->sd", hidden_all, down_w, preferred_element_type=F32).astype(BF16)
    back_out = send(expert_out.reshape(owners, tiles, LANES)).reshape(slots, columns)

    back_pre = scatter(back).astype(F32)
    grad_gate = (back_pre * up_pre * squash * (1.0 + gate_pre * (1.0 - squash))).astype(BF16)
    grad_up = (back_pre * gate_pre * squash).astype(BF16)
    inner = jnp.sum(hidden_act.astype(F32) * back_pre, axis=1)
    high = lax.reduce_precision(inner, 8, 7)
    inner_rows = jnp.stack([high, inner - high], axis=1).astype(BF16)
    inner_rows = jnp.pad(inner_rows.reshape(-1), (0, 8 * LANES - 2 * slots)).reshape(8, LANES)
    grads = jnp.concatenate([grad_gate, grad_up, inner_rows], axis=0)
    grads = lax.all_gather(grads, "ctx", axis=0, tiled=False)
    inner = jnp.sum(
        grads[:, 2 * slots :, :].reshape(parts, -1)[:, : 2 * slots].reshape(parts, slots, 2).astype(F32),
        axis=(0, 2),
    )
    event_grad = (
        jnp.einsum("ysj,dyj->sd", grads[:, :slots], gate_w, preferred_element_type=F32)
        + jnp.einsum("ysj,dyj->sd", grads[:, slots : 2 * slots], up_w, preferred_element_type=F32)
    ).astype(BF16)
    high = lax.reduce_precision(inner, 8, 7)
    extra = jnp.stack([high, inner - high], axis=1).astype(BF16).reshape(owners, 2 * capacity)
    extra = jnp.pad(extra, ((0, 0), (0, LANES - 2 * capacity)))[:, None, :]
    back_grad = send(jnp.concatenate([event_grad.reshape(owners, tiles, LANES), extra], axis=1))
    inner = jnp.sum(
        back_grad[:, tiles, : 2 * capacity].reshape(slots, 2).astype(F32), axis=1
    )
    back_grad = back_grad[:, :tiles].reshape(slots, columns)

    mixed = sum(
        event_weights[:, k][:, None] * matmul(p.astype(BF16).T, back_out) for k, p in enumerate(picks)
    ).astype(BF16)
    token_grad = matmul(pick_any.T, back_grad).astype(BF16)
    weight_grad = (
        jnp.stack([jnp.sum(jnp.where(p, inner[:, None], 0.0), axis=0) for p in picks], axis=1)
        / event_weights
    )
    return (mixed, token_grad, weight_grad)


def solution(mesh):
    in_specs = (
        P(("rep", "exp"), "ctx"),
        P(("rep", "exp"), None),
        P(("rep", "exp"), None),
        P("exp", "ctx"),
        P("exp", "ctx", None),
        P("exp", "ctx", None),
        P("exp", None, "ctx"),
    )
    out_specs = (P(("rep", "exp"), "ctx"), P(("rep", "exp"), "ctx"), P(("rep", "exp"), None))
    return jax.shard_map(shards, mesh=mesh, in_specs=in_specs, out_specs=out_specs, check_vma=False)
```

time: 385 us -> 286 us (0.74)
  the two profiles are of different devices: /device:TPU:4 before, /device:TPU:2 now
where the time goes in v1:
time: 286 us
  waiting for transfers between devices  114 us (40%)
  blocking collectives  69.5 us (24%)
  starting transfers between devices  44.8 us (16%)
  local copies, waits for them, and re-layouts  19.6 us (7%)
  matrix products  16.5 us (6%)
  between operations  14.1 us (5%)
  other arithmetic  6.86 us (2%)
    all_to_all x3, waiting for transfers between devices, send(): lax.all_to_all(buffer, 'exp', split_axis=0, concat_axis=0, tiled=True)  71.4 us
    all_to_all x3, starting transfers between devices, send(): lax.all_to_all(buffer, 'exp', split_axis=0, concat_axis=0, tiled=True)  44.7 us
    all_to_all x1, blocking collectives, send(): lax.all_to_all(buffer, 'exp', split_axis=0, concat_axis=0, tiled=True)  43.3 us
    reduce_scatter x2, waiting for transfers between devices, scatter(): return lax.psum_scatter(value, 'ctx', scatter_dimension=0, tiled=False)  40.7 us
    all_gather x1, blocking collectives, shards(): hidden_all = lax.all_gather(hidden_act, 'ctx', axis=0, tiled=False)  26.2 us
    unnamed x21, local copies, waits for them, and re-layouts  7.73 us
  transfers between devices with their start and end apart: 6, of which 5 were waited for; matrix products, arithmetic and copies ran while one was open for 9% of the time, Pallas kernels for 0%

profile of v1, /device:TPU:2, one launch (start us, length us, event | category | flops | bytes accessed | tf_op | source)
XLA Modules:
  0.0 285.6 jit_solution(15172197191397804853)
XLA Ops:
  7.2 0.9 copy.44
  9.4 1.2 convolution_convert_fusion.1
  10.6 1.4 reshape.94
  12.1 22.3 %all-to-all-start = ((bf16[64,35,128]{2,1,0:T(8,128)(2,1)}), bf16[64,35,128]{2,1,0:T(8,128)(2,1)S(1)}, u32[]{:S(2)}, u32[]{:S(2)}) async-start(bf16[64,35,128]{2,1,0:T(8,128)(2,1)} %reshape.94), calls=%async_computation | async-start | bytes 1310720 | tf_op jit(solution)/shard_map/all_to_all | solution.py:43
  34.7 1.1 fusion.26
  35.8 1.7 reshape.96
  37.5 3.4 %copy.53 = bf16[112,8,8,128]{3,2,1,0:T(8,128)(2,1)} copy(bf16[112,8,8,128]{3,1,2,0:T(8,128)(2,1)} %bitcast.85) | data formatting | bytes 3670016
  40.9 1.8 copy.54
  42.7 30.0 %all-to-all-done = bf16[64,35,128]{2,1,0:T(8,128)(2,1)S(1)} async-done(((bf16[64,35,128]{2,1,0:T(8,128)(2,1)}), bf16[64,35,128]{2,1,0:T(8,128)(2,1)S(1)}, u32[]{:S(2)}, u32[]{:S(2)}) %all-to-all-start) | async-done | bytes 573472 | tf_op jit(solution)/shard_map/all_to_all | solution.py:43
  72.7 1.4 reshape.95
  74.1 2.7 fusion.32
  77.7 1.2 pad_maximum_fusion
  78.9 43.3 %all_to_all.20 = bf16[64,35,128]{2,1,0:T(8,128)(2,1)S(1)} all-to-all(bf16[64,35,128]{2,1,0:T(8,128)(2,1)S(1)} %reshape.96), channel_id=1, replica_groups=mesh['ctx'=8,'exp'=64,'rep'=2] {'exp'}, dimensions={0} | all-to-all | bytes 1146880 | tf_op jit(solution)/shard_map/all_to_all | solution.py:43
  122.8 1.7 fusion.28
  124.6 0.9 convert_element_type.116
  125.6 40.6 %reduce-scatter.5.cloned.1.call-done = bf16[1,320,128]{2,1,0:T(8,128)(2,1)} async-done(((bf16[8,320,128]{2,1,0:T(8,128)(2,1)}), bf16[1,320,128]{2,1,0:T(8,128)(2,1)}) %reduce-scatter.5.cloned.1.call-update) | async-done | bytes 81936 | tf_op jit(solution)/shard_map/reduce_scatter | solution.py:58
  166.2 1.1 fusion.47
  168.4 26.2 %all-gather = bf16[2560,128]{1,0:T(8,128)(2,1)S(1)} all-gather(bf16[320,128]{1,0:T(8,128)(2,1)S(1)} %get-tuple-element.10), channel_id=2, replica_groups=mesh['ctx'=8,'exp'=64,'rep'=2] {'ctx'}, dimensions={0}, use_global_device_ids=true | all-gather | bytes 737280 | tf_op jit(solution)/shard_map/all_gather | solution.py:73
  195.4 1.5 reshape.97
  196.9 16.4 %all-to-all-start.1 = ((bf16[64,35,128]{2,1,0:T(8,128)(2,1)}), bf16[64,35,128]{2,1,0:T(8,128)(2,1)S(1)}, u32[]{:S(2)}, u32[]{:S(2)}) async-start(bf16[64,35,128]{2,1,0:T(8,128)(2,1)} %reshape.97), calls=%async_computation.2 | async-start | bytes 1310720 | tf_op jit(solution)/shard_map/all_to_all | solution.py:43
  213.3 2.1 all-gather.4.cloned.1.call-done
  216.1 2.7 fusion.8
  218.9 2.8 fusion.23
  221.7 1.7 reshape.101
  224.1 0.9 pad_maximum_fusion.1
  225.0 15.2 %all-to-all-done.1 = bf16[64,35,128]{2,1,0:T(8,128)(2,1)S(1)} async-done(((bf16[64,35,128]{2,1,0:T(8,128)(2,1)}), bf16[64,35,128]{2,1,0:T(8,128)(2,1)S(1)}, u32[]{:S(2)}, u32[]{:S(2)}) %all-to-all-start.1) | async-done | bytes 573472 | tf_op jit(solution)/shard_map/all_to_all | solution.py:43
  240.2 0.9 copy-done.1
  241.1 6.0 %all-to-all-start.3 = ((bf16[64,36,128]{2,1,0:T(8,128)(2,1)}), bf16[64,36,128]{2,1,0:T(8,128)(2,1)S(1)}, u32[]{:S(2)}, u32[]{:S(2)}) async-start(bf16[64,36,128]{2,1,0:T(8,128)(2,1)} %pad_maximum_fusion.1), calls=%async_computation.5 | async-start | bytes 1310720 | tf_op jit(solution)/shard_map/all_to_all | solution.py:43
  247.0 1.8 reshape.98
  249.2 1.0 fusion.36
  250.2 26.2 %all-to-all-done.3 = bf16[64,36,128]{2,1,0:T(8,128)(2,1)S(1)} async-done(((bf16[64,36,128]{2,1,0:T(8,128)(2,1)}), bf16[64,36,128]{2,1,0:T(8,128)(2,1)S(1)}, u32[]{:S(2)}, u32[]{:S(2)}) %all-to-all-start.3) | async-done | bytes 589856 | tf_op jit(solution)/shard_map/all_to_all | solution.py:43
  277.5 1.0 convolution_convert_fusion.2
  (59 shorter events, 8.4 us)
Async XLA Ops:
  7.2 115.6 %copy-start = (bf16[1,1024,896]{2,1,0:T(8,128)(2,1)S(1)}, bf16[1,1024,896]{2,1,0:T(8,128)(2,1)}, u32[]{:S(2)}) copy-start(bf16[1,1024,896]{2,1,0:T(8,128)(2,1)} %param.13) | copy-start | bytes 5505028
  8.1 26.3 %copy-start.7 = (f32[128,2]{0,1:T(2,128)S(1)}, f32[128,2]{0,1:T(2,128)}, u32[]{:S(2)}) copy-start(f32[128,2]{0,1:T(2,128)} %param.9) | copy-start | bytes 3076
  8.2 26.4 %copy-start.6 = (bf16[128,896]{1,0:T(8,128)(2,1)S(1)}, bf16[128,896]{1,0:T(8,128)(2,1)}, u32[]{:S(2)}) copy-start(bf16[128,896]{1,0:T(8,128)(2,1)} %param.10) | copy-start | bytes 688132
  12.1 60.6 %all-to-all-start = ((bf16[64,35,128]{2,1,0:T(8,128)(2,1)}), bf16[64,35,128]{2,1,0:T(8,128)(2,1)S(1)}, u32[]{:S(2)}, u32[]{:S(2)}) async-start(bf16[64,35,128]{2,1,0:T(8,128)(2,1)} %reshape.94), calls=%async_computation | async-start | bytes 1310720 | tf_op jit(solution)/shard_map/all_to_all | solution.py:43
  34.4 90.2 %reduce-scatter.3.cloned.1.call-start = ((), (), s32[]{:S(2)}) async-start(), calls=%async_computation.6 | async-start | bytes 1474560 | tf_op jit(solution)/shard_map/reduce_scatter | solution.py:58
  37.5 3.4 %copy-start.2 = (bf16[1,896,1024]{2,1,0:T(8,128)(2,1)S(1)}, bf16[1,896,1024]{2,1,0:T(8,128)(2,1)}, u32[]{:S(2)}) copy-start(bf16[1,896,1024]{2,1,0:T(8,128)(2,1)} %param.12) | copy-start | bytes 5505028
  74.1 2.7 copy-start.3
  74.1 2.7 copy-start.5
  78.8 87.4 %reduce-scatter.5.cloned.1.call-start = ((), (), s32[]{:S(2)}) async-start(), calls=%async_computation.7 | async-start | bytes 737280 | tf_op jit(solution)/shard_map/reduce_scatter | solution.py:58
  124.5 90.8 %all-gather.4.cloned.1.call-start = ((), (), s32[]{:S(2)}) async-start(), calls=%async_computation.8 | async-start | bytes 1492992 | tf_op jit(solution)/shard_map/all_gather | solution.py:85
  196.9 43.3 %all-to-all-start.1 = ((bf16[64,35,128]{2,1,0:T(8,128)(2,1)}), bf16[64,35,128]{2,1,0:T(8,128)(2,1)S(1)}, u32[]{:S(2)}, u32[]{:S(2)}) async-start(bf16[64,35,128]{2,1,0:T(8,128)(2,1)} %reshape.97), calls=%async_computation.2 | async-start | bytes 1310720 | tf_op jit(solution)/shard_map/all_to_all | solution.py:43
  216.1 2.7 copy-start.4
  240.2 0.9 copy-start.1
  241.1 35.3 %all-to-all-start.3 = ((bf16[64,36,128]{2,1,0:T(8,128)(2,1)}), bf16[64,36,128]{2,1,0:T(8,128)(2,1)S(1)}, u32[]{:S(2)}, u32[]{:S(2)}) async-start(bf16[64,36,128]{2,1,0:T(8,128)(2,1)} %pad_maximum_fusion.1), calls=%async_computation.5 | async-start | bytes 1310720 | tf_op jit(solution)/shard_map/all_to_all | solution.py:43
Sparse Core Ops, SparseCore 0:
  79.0 38.7 reduce-scatter.2
  124.7 41.5 reduce-scatter.4
  169.5 45.8 all-gather.3

commit v2 on v1

v2 whole, which is shorter than its diff:
```python
import jax
import jax.numpy as jnp
from jax import lax
from jax.sharding import PartitionSpec as P


LANES = 128
F32 = jnp.float32
BF16 = jnp.bfloat16


def matmul(a, b):
    return jnp.dot(a, b, preferred_element_type=F32)


def experts(tokens, routes, event_weights, cotangent, w_gate, w_up, w_down):
    owners = lax.axis_size("exp")
    parts = lax.axis_size("ctx")
    rows, fanout = routes.shape
    _, columns, hidden = w_gate.shape
    capacity = max(2, 5 * rows * fanout // (4 * owners))
    slots = owners * capacity
    piece = hidden // parts
    tiles = capacity * columns // LANES

    flat = routes.reshape(-1)
    named = (flat[:, None] == jnp.arange(owners, dtype=jnp.int32)[None, :]).astype(BF16)
    events = rows * fanout
    earlier = (
        jnp.arange(events)[:, None] > jnp.arange(events)[None, :]
    ).astype(BF16)
    before = matmul(earlier, named)
    places = jnp.sum(before * named.astype(F32), axis=1).astype(jnp.int32)
    targets = (flat * capacity + places).reshape(rows, fanout)
    slot_ids = jnp.arange(slots, dtype=jnp.int32)
    picks = [slot_ids[:, None] == targets[:, k][None, :] for k in range(fanout)]
    pick_any = sum(p.astype(BF16) for p in picks)
    slot_weights = sum(
        jnp.sum(jnp.where(p, event_weights[:, k][None, :], 0.0), axis=1)
        for k, p in enumerate(picks)
    )

    me = lax.axis_index("ctx")

    def send(buffer):
        return lax.all_to_all(buffer, "exp", split_axis=0, concat_axis=0, tiled=True)

    def block(value, step):
        return lax.squeeze(lax.dynamic_slice_in_dim(value, lax.rem(me + step, parts), 1, 0), (0,))

    def shifted(value, step):
        return lax.ppermute(value, "ctx", [(i, (i + step) % parts) for i in range(parts)])

    steps = sorted(range(1, parts), key=lambda step: (min(step, parts - step), step))

    send_tokens = matmul(pick_any, tokens).astype(BF16).reshape(owners, tiles, LANES)
    recv_tokens = send(send_tokens)
    send_cots = (
        (slot_weights[:, None] * matmul(pick_any, cotangent)).astype(BF16).reshape(owners, tiles, LANES)
    )
    gate_w = w_gate[0].reshape(columns, parts, piece).transpose(1, 0, 2)
    up_w = w_up[0].reshape(columns, parts, piece).transpose(1, 0, 2)
    recv_tokens, send_cots, gate_w, up_w = lax.optimization_barrier(
        (recv_tokens, send_cots, gate_w, up_w)
    )
    recv_cots = send(send_cots)
    expert_in = recv_tokens.reshape(slots, columns)
    expert_cot = recv_cots.reshape(slots, columns)

    down_w = w_down[0].reshape(parts, piece, columns)

    gate_up = jnp.concatenate(
        [
            jnp.einsum("sd,ydj->ysj", expert_in, gate_w, preferred_element_type=F32).astype(BF16),
            jnp.einsum("sd,ydj->ysj", expert_in, up_w, preferred_element_type=F32).astype(BF16),
        ],
        axis=1,
    )
    arrived = [shifted(block(gate_up, step), step) for step in steps]
    gate_up = sum((a.astype(F32) for a in arrived), block(gate_up, 0).astype(F32))
    gate_pre, up_pre = gate_up[:slots], gate_up[slots:]
    squash = jax.nn.sigmoid(gate_pre)
    hidden_act = (gate_pre * squash * up_pre).astype(BF16)

    back = jnp.einsum("sd,yjd->ysj", expert_cot, down_w, preferred_element_type=F32).astype(BF16)
    hidden_act, back = lax.optimization_barrier((hidden_act, back))
    back = lax.all_to_all(back, "ctx", split_axis=0, concat_axis=0, tiled=True)
    hidden_all = lax.all_gather(hidden_act, "ctx", axis=0, tiled=False)
    expert_out = jnp.einsum("ysj,yjd->sd", hidden_all, down_w, preferred_element_type=F32).astype(BF16)
    back, send_out = lax.optimization_barrier((back, expert_out.reshape(owners, tiles, LANES)))
    back_out = send(send_out)

    back_pre = jnp.sum(back.astype(F32), axis=0)
    grad_gate = (back_pre * up_pre * squash * (1.0 + gate_pre * (1.0 - squash))).astype(BF16)
    grad_up = (back_pre * gate_pre * squash).astype(BF16)
    inner = jnp.sum(hidden_act.astype(F32) * back_pre, axis=1)
    high = lax.reduce_precision(inner, 8, 7)
    inner_rows = jnp.stack([high, inner - high], axis=0).astype(BF16)
    inner_rows = jnp.pad(inner_rows.reshape(-1), (0, 8 * LANES - 2 * slots)).reshape(8, LANES)
    grads = jnp.concatenate([grad_gate, grad_up, inner_rows], axis=0)
    arrived = [shifted(grads, -step) for step in steps]
    gathered = jnp.zeros((parts, *grads.shape), BF16)
    for step, value in zip([0, *steps], [grads, *arrived]):
        gathered = lax.dynamic_update_slice(gathered, value[None], (lax.rem(me + step, parts), 0, 0))
    grads = gathered
    inner = jnp.sum(grads[:, 2 * slots :, :].reshape(parts, -1).astype(F32), axis=0)
    inner = inner[:slots] + inner[slots : 2 * slots]
    event_grad = (
        jnp.einsum("ysj,ydj->sd", grads[:, :slots], gate_w, preferred_element_type=F32)
        + jnp.einsum("ysj,ydj->sd", grads[:, slots : 2 * slots], up_w, preferred_element_type=F32)
    ).astype(BF16)
    high = lax.reduce_precision(inner, 8, 7)
    extra = jnp.concatenate(
        [high.reshape(owners, capacity), (inner - high).reshape(owners, capacity)], axis=1
    ).astype(BF16)
    extra = jnp.pad(extra, ((0, 0), (0, LANES - 2 * capacity)))[:, None, :]
    back_grad = send(jnp.concatenate([event_grad.reshape(owners, tiles, LANES), extra], axis=1))
    back_out = back_out.reshape(slots, columns)
    extra = back_grad[:, tiles, : 2 * capacity].astype(F32)
    inner = (extra[:, :capacity] + extra[:, capacity:]).reshape(slots)
    back_grad = back_grad[:, :tiles].reshape(slots, columns)

    mixed = sum(
        event_weights[:, k][:, None] * matmul(p.astype(BF16).T, back_out) for k, p in enumerate(picks)
    ).astype(BF16)
    token_grad = matmul(pick_any.T, back_grad).astype(BF16)
    weight_grad = (
        jnp.stack([jnp.sum(jnp.where(p, inner[:, None], 0.0), axis=0) for p in picks], axis=1)
        / event_weights
    )
    return (mixed, token_grad, weight_grad)


def solution(mesh):
    in_specs = (
        P(("rep", "exp"), "ctx"),
        P(("rep", "exp"), None),
        P(("rep", "exp"), None),
        P("exp", "ctx"),
        P("exp", "ctx", None),
        P("exp", "ctx", None),
        P("exp", None, "ctx"),
    )
    out_specs = (P(("rep", "exp"), "ctx"), P(("rep", "exp"), "ctx"), P(("rep", "exp"), None))
    return jax.shard_map(experts, mesh=mesh, in_specs=in_specs, out_specs=out_specs, check_vma=False)
```

time: 286 us -> 283 us (0.990)
  starting transfers between devices: 44.8 us -> 121 us
  waiting for transfers between devices: 114 us -> 76.8 us
  blocking collectives: 69.5 us -> 37.1 us
  between operations: 14.1 us -> 1.27 us
  local copies, waits for them, and re-layouts: 19.6 us -> 22.7 us
    ppermute x0 -> x14, starting transfers between devices: none -> 59.3 us  [shifted(): lax.ppermute(value, 'ctx', [(i, (i + step) % parts) for i in range(parts)])]
    all_to_all x1 -> x0, blocking collectives: 43.3 us -> none  [send(): lax.all_to_all(buffer, 'exp', split_axis=0, concat_axis=0, tiled=True)]
    reduce_scatter x2 -> x0, waiting for transfers between devices: 40.7 us -> none  [scatter(): return lax.psum_scatter(value, 'ctx', scatter_dimension=0, tiled=False)]
    ppermute x0 -> x14, waiting for transfers between devices: none -> 15.5 us  [shifted(): lax.ppermute(value, 'ctx', [(i, (i + step) % parts) for i in range(parts)])]
    all_to_all x3 -> x4, starting transfers between devices: 44.7 us -> 57.5 us  [send(): lax.all_to_all(buffer, 'exp', split_axis=0, concat_axis=0, tiled=True)]
    all_gather x1, blocking collectives: 26.2 us -> 37.1 us  [experts(): hidden_all = lax.all_gather(hidden_act, 'ctx', axis=0, tiled=False)]
    all_to_all x3 -> x4, waiting for transfers between devices: 71.4 us -> 61.3 us  [send(): lax.all_to_all(buffer, 'exp', split_axis=0, concat_axis=0, tiled=True)]
    all_to_all x0 -> x1, starting transfers between devices: none -> 4.6 us  [experts(): back = lax.all_to_all(back, 'ctx', split_axis=0, concat_axis=0, tiled=True)]
  transfers between devices with their start and end apart: 6 -> 19, of which waited for: 5 -> 8; matrix products, arithmetic and copies ran while one was open for 9% -> 11% of each run, Pallas kernels for 0% -> 0%
where the time goes in v2:
time: 283 us; the launch traced here: 282 us
  starting transfers between devices  121 us (43%)
  waiting for transfers between devices  76.8 us (27%)
  blocking collectives  37.1 us (13%)
  local copies, waits for them, and re-layouts  22.7 us (8%)
  matrix products  17.4 us (6%)
  other arithmetic  5.54 us (2%)
    all_to_all x4, waiting for transfers between devices, send(): lax.all_to_all(buffer, 'exp', split_axis=0, concat_axis=0, tiled=True)  61.3 us
    ppermute x14, starting transfers between devices, shifted(): lax.ppermute(value, 'ctx', [(i, (i + step) % parts) for i in range(parts)])  59.3 us
    all_to_all x4, starting transfers between devices, send(): lax.all_to_all(buffer, 'exp', split_axis=0, concat_axis=0, tiled=True)  57.5 us
    all_gather x1, blocking collectives, experts(): hidden_all = lax.all_gather(hidden_act, 'ctx', axis=0, tiled=False)  37.1 us
    ppermute x14, waiting for transfers between devices, shifted(): lax.ppermute(value, 'ctx', [(i, (i + step) % parts) for i in range(parts)])  15.5 us
    unnamed x23, local copies, waits for them, and re-layouts  6.38 us
  transfers between devices with their start and end apart: 19, of which 8 were waited for; matrix products, arithmetic and copies ran while one was open for 11% of the time, Pallas kernels for 0%

profile of v2, /device:TPU:2, one launch (start us, length us, event | category | flops | bytes accessed | tf_op | source)
XLA Modules:
  0.0 282.2 jit_solution(252429285760811796)
XLA Ops:
  5.6 22.3 %all-to-all-start = ((bf16[64,35,128]{2,1,0:T(8,128)(2,1)}), bf16[64,35,128]{2,1,0:T(8,128)(2,1)S(1)}, u32[]{:S(2)}, u32[]{:S(2)}) async-start(bf16[64,35,128]{2,1,0:T(8,128)(2,1)} %reshape.78), calls=%async_computation | async-start | bytes 1310720 | tf_op jit(solution)/shard_map/all_to_all | solution.py:46
  29.8 2.2 copy.50
  32.6 2.4 copy_bitcast_fusion
  35.0 31.2 %all-to-all-done = bf16[64,35,128]{2,1,0:T(8,128)(2,1)S(1)} async-done(((bf16[64,35,128]{2,1,0:T(8,128)(2,1)}), bf16[64,35,128]{2,1,0:T(8,128)(2,1)S(1)}, u32[]{:S(2)}, u32[]{:S(2)}) %all-to-all-start) | async-done | bytes 573472 | tf_op jit(solution)/shard_map/all_to_all | solution.py:46
  66.2 6.1 %all-to-all-start.1 = ((bf16[64,35,128]{2,1,0:T(8,128)(2,1)}), bf16[64,35,128]{2,1,0:T(8,128)(2,1)}, u32[]{:S(2)}, u32[]{:S(2)}) async-start(bf16[64,35,128]{2,1,0:T(8,128)(2,1)} %reshape.79), calls=%async_computation.1 | async-start | bytes 1310720 | tf_op jit(solution)/shard_map/all_to_all | solution.py:46
  73.8 2.5 fusion.6
  76.3 1.9 fusion.5
  78.2 7.7 %collective-permute-start.6 = (bf16[640,128]{1,0:T(8,128)(2,1)S(1)}, bf16[640,128]{1,0:T(8,128)(2,1)}, u32[]{:S(2)}, u32[]{:S(2)}) collective-permute-start(bf16[640,128]{1,0:T(8,128)(2,1)S(1)} %fusion.34), channel_id=1, source_target_pairs={{0,512},{128,640},{256,768},{384,896},{512,0},{640,128},{768,256},... | collective-permute-start | bytes 491528 | tf_op jit(solution)/shard_map/ppermute | solution.py:52
  86.8 2.1 collective-permute-start.5
  89.0 5.5 %collective-permute-start.4 = (bf16[640,128]{1,0:T(8,128)(2,1)}, bf16[640,128]{1,0:T(8,128)(2,1)S(1)}, u32[]{:S(2)}, u32[]{:S(2)}) collective-permute-start(bf16[640,128]{1,0:T(8,128)(2,1)} %get-tuple-element.25), channel_id=1, source_target_pairs={{0,384},{128,512},{256,640},{384,768},{512,896},{640,0},{768,128},... | collective-permute-start | bytes 491528 | tf_op jit(solution)/shard_map/ppermute | solution.py:52
  94.5 3.5 %collective-permute-start.3 = (bf16[640,128]{1,0:T(8,128)(2,1)}, bf16[640,128]{1,0:T(8,128)(2,1)}, u32[]{:S(2)}, u32[]{:S(2)}) collective-permute-start(bf16[640,128]{1,0:T(8,128)(2,1)} %get-tuple-element.24), channel_id=1, source_target_pairs={{0,768},{128,896},{256,0},{384,128},{512,256},{640,384},{768,512},... | collective-permute-start | bytes 491528 | tf_op jit(solution)/shard_map/ppermute | solution.py:52
  97.9 3.3 %collective-permute-start.2 = (bf16[640,128]{1,0:T(8,128)(2,1)}, bf16[640,128]{1,0:T(8,128)(2,1)}, u32[]{:S(2)}, u32[]{:S(2)}) collective-permute-start(bf16[640,128]{1,0:T(8,128)(2,1)} %get-tuple-element.23), channel_id=1, source_target_pairs={{0,256},{128,384},{256,512},{384,640},{512,768},{640,896},{768,0},... | collective-permute-start | bytes 491528 | tf_op jit(solution)/shard_map/ppermute | solution.py:52
  101.2 4.8 %collective-permute-start.1 = (bf16[640,128]{1,0:T(8,128)(2,1)}, bf16[640,128]{1,0:T(8,128)(2,1)}, u32[]{:S(2)}, u32[]{:S(2)}) collective-permute-start(bf16[640,128]{1,0:T(8,128)(2,1)} %get-tuple-element.22), channel_id=1, source_target_pairs={{0,896},{128,0},{256,128},{384,256},{512,384},{640,512},{768,640},... | collective-permute-start | bytes 491528 | tf_op jit(solution)/shard_map/ppermute | solution.py:52
  106.0 5.5 %collective-permute-start = (bf16[640,128]{1,0:T(8,128)(2,1)S(1)}, bf16[640,128]{1,0:T(8,128)(2,1)}, u32[]{:S(2)}, u32[]{:S(2)}) collective-permute-start(bf16[640,128]{1,0:T(8,128)(2,1)S(1)} %get-tuple-element.21), channel_id=1, source_target_pairs={{0,128},{128,256},{256,384},{384,512},{512,640},{640,768},{768,896... | collective-permute-start | bytes 491528 | tf_op jit(solution)/shard_map/ppermute | solution.py:52
  117.5 1.8 reshape.91
  120.9 4.6 %all-to-all-start.2 = ((bf16[8,320,128]{2,1,0:T(8,128)(2,1)}), bf16[8,320,128]{2,1,0:T(8,128)(2,1)S(1)}, u32[]{:S(2)}, u32[]{:S(2)}) async-start(bf16[8,320,128]{2,1,0:T(8,128)(2,1)} %fusion.4), calls=%async_computation.2 | async-start | bytes 1310720 | tf_op jit(solution)/shard_map/all_to_all | solution.py:87
  125.6 37.1 %all-gather = bf16[2560,128]{1,0:T(8,128)(2,1)S(1)} all-gather(bf16[320,128]{1,0:T(8,128)(2,1)S(1)} %multiply_convert_fusion.2), channel_id=2, replica_groups=mesh['ctx'=8,'exp'=64,'rep'=2] {'ctx'}, dimensions={0}, use_global_device_ids=true | all-gather | bytes 737280 | tf_op jit(solution)/shard_map/all_gather | solution.py:88
  164.4 2.5 reshape.82
  167.2 3.9 %collective-permute-start.7 = (bf16[648,128]{1,0:T(8,128)(2,1)S(1)}, bf16[648,128]{1,0:T(8,128)(2,1)}, u32[]{:S(2)}, u32[]{:S(2)}) collective-permute-start(bf16[648,128]{1,0:T(8,128)(2,1)S(1)} %pad_maximum_fusion.1), channel_id=1, source_target_pairs={{0,896},{128,0},{256,128},{384,256},{512,384},{640,512},{768,640},... | collective-permute-start | bytes 497672 | tf_op jit(solution)/shard_map/ppermute | solution.py:52
  171.1 1.9 collective-permute-start.8
  173.1 4.6 %collective-permute-start.9 = (bf16[648,128]{1,0:T(8,128)(2,1)S(1)}, bf16[648,128]{1,0:T(8,128)(2,1)S(1)}, u32[]{:S(2)}, u32[]{:S(2)}) collective-permute-start(bf16[648,128]{1,0:T(8,128)(2,1)S(1)} %pad_maximum_fusion.1), channel_id=1, source_target_pairs={{0,768},{128,896},{256,0},{384,128},{512,256},{640,384},{768,512},... | collective-permute-start | bytes 497672 | tf_op jit(solution)/shard_map/ppermute | solution.py:52
  177.7 2.2 collective-permute-start.10
  179.9 7.0 %collective-permute-start.11 = (bf16[648,128]{1,0:T(8,128)(2,1)S(1)}, bf16[648,128]{1,0:T(8,128)(2,1)S(1)}, u32[]{:S(2)}, u32[]{:S(2)}) collective-permute-start(bf16[648,128]{1,0:T(8,128)(2,1)S(1)} %pad_maximum_fusion.1), channel_id=1, source_target_pairs={{0,640},{128,768},{256,896},{384,0},{512,128},{640,256},{768,384},... | collective-permute-start | bytes 497672 | tf_op jit(solution)/shard_map/ppermute | solution.py:52
  186.8 15.3 %all-to-all-start.3 = ((bf16[64,35,128]{2,1,0:T(8,128)(2,1)}), bf16[64,35,128]{2,1,0:T(8,128)(2,1)S(1)}, u32[]{:S(2)}, u32[]{:S(2)}) async-start(bf16[64,35,128]{2,1,0:T(8,128)(2,1)} %reshape.82), calls=%async_computation.3 | async-start | bytes 1310720 | tf_op jit(solution)/shard_map/all_to_all | solution.py:46
  202.4 3.4 %collective-permute-start.12 = (bf16[648,128]{1,0:T(8,128)(2,1)S(1)}, bf16[648,128]{1,0:T(8,128)(2,1)S(1)}, u32[]{:S(2)}, u32[]{:S(2)}) collective-permute-start(bf16[648,128]{1,0:T(8,128)(2,1)S(1)} %pad_maximum_fusion.1), channel_id=1, source_target_pairs={{0,384},{128,512},{256,640},{384,768},{512,896},{640,0},{768,128},... | collective-permute-start | bytes 497672 | tf_op jit(solution)/shard_map/ppermute | solution.py:52
  206.7 4.0 %collective-permute-start.13 = (bf16[648,128]{1,0:T(8,128)(2,1)S(1)}, bf16[648,128]{1,0:T(8,128)(2,1)S(1)}, u32[]{:S(2)}, u32[]{:S(2)}) collective-permute-start(bf16[648,128]{1,0:T(8,128)(2,1)S(1)} %pad_maximum_fusion.1), channel_id=1, source_target_pairs={{0,512},{128,640},{256,768},{384,896},{512,0},{640,128},{768,256},... | collective-permute-start | bytes 497672 | tf_op jit(solution)/shard_map/ppermute | solution.py:52
  210.8 5.9 %collective-permute-done.12 = bf16[648,128]{1,0:T(8,128)(2,1)S(1)} collective-permute-done((bf16[648,128]{1,0:T(8,128)(2,1)S(1)}, bf16[648,128]{1,0:T(8,128)(2,1)S(1)}, u32[]{:S(2)}, u32[]{:S(2)}) %collective-permute-start.12) | collective-permute-done | bytes 165920 | tf_op jit(solution)/shard_map/ppermute | solution.py:52
  216.8 5.2 %collective-permute-done.13 = bf16[648,128]{1,0:T(8,128)(2,1)S(1)} collective-permute-done((bf16[648,128]{1,0:T(8,128)(2,1)S(1)}, bf16[648,128]{1,0:T(8,128)(2,1)S(1)}, u32[]{:S(2)}, u32[]{:S(2)}) %collective-permute-start.13) | collective-permute-done | bytes 165920 | tf_op jit(solution)/shard_map/ppermute | solution.py:52
  223.6 2.7 convolution_bitcast_fusion
  226.3 2.8 fusion.1
  233.9 13.8 %all-to-all-start.4 = ((bf16[64,36,128]{2,1,0:T(8,128)(2,1)}), bf16[64,36,128]{2,1,0:T(8,128)(2,1)S(1)}, u32[]{:S(2)}, u32[]{:S(2)}) async-start(bf16[64,36,128]{2,1,0:T(8,128)(2,1)} %pad_maximum_fusion), calls=%async_computation.4 | async-start | bytes 1310720 | tf_op jit(solution)/shard_map/all_to_all | solution.py:46
  250.9 28.8 %all-to-all-done.4 = bf16[64,36,128]{2,1,0:T(8,128)(2,1)S(1)} async-done(((bf16[64,36,128]{2,1,0:T(8,128)(2,1)}), bf16[64,36,128]{2,1,0:T(8,128)(2,1)S(1)}, u32[]{:S(2)}, u32[]{:S(2)}) %all-to-all-start.4) | async-done | bytes 589856 | tf_op jit(solution)/shard_map/all_to_all | solution.py:46
  (93 shorter events, 32.7 us)
Async XLA Ops:
  0.6 118.6 %copy-start = (bf16[1,1024,896]{2,1,0:T(8,128)(2,1)S(1)}, bf16[1,1024,896]{2,1,0:T(8,128)(2,1)}, u32[]{:S(2)}) copy-start(bf16[1,1024,896]{2,1,0:T(8,128)(2,1)} %param.13) | copy-start | bytes 5505028
  4.1 23.8 %copy-start.9 = (f32[128,2]{0,1:T(2,128)S(1)}, f32[128,2]{0,1:T(2,128)}, u32[]{:S(2)}) copy-start(f32[128,2]{0,1:T(2,128)} %param.9) | copy-start | bytes 3076
  4.1 24.0 %copy-start.7 = (bf16[128,896]{1,0:T(8,128)(2,1)S(1)}, bf16[128,896]{1,0:T(8,128)(2,1)}, u32[]{:S(2)}) copy-start(bf16[128,896]{1,0:T(8,128)(2,1)} %param.10) | copy-start | bytes 688132
  5.6 60.6 %all-to-all-start = ((bf16[64,35,128]{2,1,0:T(8,128)(2,1)}), bf16[64,35,128]{2,1,0:T(8,128)(2,1)S(1)}, u32[]{:S(2)}, u32[]{:S(2)}) async-start(bf16[64,35,128]{2,1,0:T(8,128)(2,1)} %reshape.78), calls=%async_computation | async-start | bytes 1310720 | tf_op jit(solution)/shard_map/all_to_all | solution.py:46
  29.8 2.2 copy-start.4
  66.2 51.3 %all-to-all-start.1 = ((bf16[64,35,128]{2,1,0:T(8,128)(2,1)}), bf16[64,35,128]{2,1,0:T(8,128)(2,1)}, u32[]{:S(2)}, u32[]{:S(2)}) async-start(bf16[64,35,128]{2,1,0:T(8,128)(2,1)} %reshape.79), calls=%async_computation.1 | async-start | bytes 1310720 | tf_op jit(solution)/shard_map/all_to_all | solution.py:46
  73.0 0.8 copy-start.6
  73.8 2.5 copy-start.2
  78.2 23.0 %collective-permute-start.6 = (bf16[640,128]{1,0:T(8,128)(2,1)S(1)}, bf16[640,128]{1,0:T(8,128)(2,1)}, u32[]{:S(2)}, u32[]{:S(2)}) collective-permute-start(bf16[640,128]{1,0:T(8,128)(2,1)S(1)} %fusion.34), channel_id=1, source_target_pairs={{0,512},{128,640},{256,768},{384,896},{512,0},{640,128},{768,256},... | collective-permute-start | bytes 491528 | tf_op jit(solution)/shard_map/ppermute | solution.py:52
  86.8 19.2 %collective-permute-start.5 = (bf16[640,128]{1,0:T(8,128)(2,1)S(1)}, bf16[640,128]{1,0:T(8,128)(2,1)}, u32[]{:S(2)}, u32[]{:S(2)}) collective-permute-start(bf16[640,128]{1,0:T(8,128)(2,1)S(1)} %get-tuple-element.26), channel_id=1, source_target_pairs={{0,640},{128,768},{256,896},{384,0},{512,128},{640,256},{768,384},... | collective-permute-start | bytes 491528 | tf_op jit(solution)/shard_map/ppermute | solution.py:52
  89.0 22.6 %collective-permute-start.4 = (bf16[640,128]{1,0:T(8,128)(2,1)}, bf16[640,128]{1,0:T(8,128)(2,1)S(1)}, u32[]{:S(2)}, u32[]{:S(2)}) collective-permute-start(bf16[640,128]{1,0:T(8,128)(2,1)} %get-tuple-element.25), channel_id=1, source_target_pairs={{0,384},{128,512},{256,640},{384,768},{512,896},{640,0},{768,128},... | collective-permute-start | bytes 491528 | tf_op jit(solution)/shard_map/ppermute | solution.py:52
  94.5 17.1 %collective-permute-start.3 = (bf16[640,128]{1,0:T(8,128)(2,1)}, bf16[640,128]{1,0:T(8,128)(2,1)}, u32[]{:S(2)}, u32[]{:S(2)}) collective-permute-start(bf16[640,128]{1,0:T(8,128)(2,1)} %get-tuple-element.24), channel_id=1, source_target_pairs={{0,768},{128,896},{256,0},{384,128},{512,256},{640,384},{768,512},... | collective-permute-start | bytes 491528 | tf_op jit(solution)/shard_map/ppermute | solution.py:52
  97.9 15.0 %collective-permute-start.2 = (bf16[640,128]{1,0:T(8,128)(2,1)}, bf16[640,128]{1,0:T(8,128)(2,1)}, u32[]{:S(2)}, u32[]{:S(2)}) collective-permute-start(bf16[640,128]{1,0:T(8,128)(2,1)} %get-tuple-element.23), channel_id=1, source_target_pairs={{0,256},{128,384},{256,512},{384,640},{512,768},{640,896},{768,0},... | collective-permute-start | bytes 491528 | tf_op jit(solution)/shard_map/ppermute | solution.py:52
  101.2 12.9 %collective-permute-start.1 = (bf16[640,128]{1,0:T(8,128)(2,1)}, bf16[640,128]{1,0:T(8,128)(2,1)}, u32[]{:S(2)}, u32[]{:S(2)}) collective-permute-start(bf16[640,128]{1,0:T(8,128)(2,1)} %get-tuple-element.22), channel_id=1, source_target_pairs={{0,896},{128,0},{256,128},{384,256},{512,384},{640,512},{768,640},... | collective-permute-start | bytes 491528 | tf_op jit(solution)/shard_map/ppermute | solution.py:52
  106.0 9.9 %collective-permute-start = (bf16[640,128]{1,0:T(8,128)(2,1)S(1)}, bf16[640,128]{1,0:T(8,128)(2,1)}, u32[]{:S(2)}, u32[]{:S(2)}) collective-permute-start(bf16[640,128]{1,0:T(8,128)(2,1)S(1)} %get-tuple-element.21), channel_id=1, source_target_pairs={{0,128},{128,256},{256,384},{384,512},{512,640},{640,768},{768,896... | collective-permute-start | bytes 491528 | tf_op jit(solution)/shard_map/ppermute | solution.py:52
  111.6 2.6 copy-start.8
  120.9 45.9 %all-to-all-start.2 = ((bf16[8,320,128]{2,1,0:T(8,128)(2,1)}), bf16[8,320,128]{2,1,0:T(8,128)(2,1)S(1)}, u32[]{:S(2)}, u32[]{:S(2)}) async-start(bf16[8,320,128]{2,1,0:T(8,128)(2,1)} %fusion.4), calls=%async_computation.2 | async-start | bytes 1310720 | tf_op jit(solution)/shard_map/all_to_all | solution.py:87
  167.2 35.1 %collective-permute-start.7 = (bf16[648,128]{1,0:T(8,128)(2,1)S(1)}, bf16[648,128]{1,0:T(8,128)(2,1)}, u32[]{:S(2)}, u32[]{:S(2)}) collective-permute-start(bf16[648,128]{1,0:T(8,128)(2,1)S(1)} %pad_maximum_fusion.1), channel_id=1, source_target_pairs={{0,896},{128,0},{256,128},{384,256},{512,384},{640,512},{768,640},... | collective-permute-start | bytes 497672 | tf_op jit(solution)/shard_map/ppermute | solution.py:52
  171.1 35.5 %collective-permute-start.8 = (bf16[648,128]{1,0:T(8,128)(2,1)S(1)}, bf16[648,128]{1,0:T(8,128)(2,1)S(1)}, u32[]{:S(2)}, u32[]{:S(2)}) collective-permute-start(bf16[648,128]{1,0:T(8,128)(2,1)S(1)} %pad_maximum_fusion.1), channel_id=1, source_target_pairs={{0,128},{128,256},{256,384},{384,512},{512,640},{640,768},{768,896... | collective-permute-start | bytes 497672 | tf_op jit(solution)/shard_map/ppermute | solution.py:52
  173.1 37.6 %collective-permute-start.9 = (bf16[648,128]{1,0:T(8,128)(2,1)S(1)}, bf16[648,128]{1,0:T(8,128)(2,1)S(1)}, u32[]{:S(2)}, u32[]{:S(2)}) collective-permute-start(bf16[648,128]{1,0:T(8,128)(2,1)S(1)} %pad_maximum_fusion.1), channel_id=1, source_target_pairs={{0,768},{128,896},{256,0},{384,128},{512,256},{640,384},{768,512},... | collective-permute-start | bytes 497672 | tf_op jit(solution)/shard_map/ppermute | solution.py:52
  177.7 33.1 %collective-permute-start.10 = (bf16[648,128]{1,0:T(8,128)(2,1)S(1)}, bf16[648,128]{1,0:T(8,128)(2,1)S(1)}, u32[]{:S(2)}, u32[]{:S(2)}) collective-permute-start(bf16[648,128]{1,0:T(8,128)(2,1)S(1)} %pad_maximum_fusion.1), channel_id=1, source_target_pairs={{0,256},{128,384},{256,512},{384,640},{512,768},{640,896},{768,0},... | collective-permute-start | bytes 497672 | tf_op jit(solution)/shard_map/ppermute | solution.py:52
  179.9 30.9 %collective-permute-start.11 = (bf16[648,128]{1,0:T(8,128)(2,1)S(1)}, bf16[648,128]{1,0:T(8,128)(2,1)S(1)}, u32[]{:S(2)}, u32[]{:S(2)}) collective-permute-start(bf16[648,128]{1,0:T(8,128)(2,1)S(1)} %pad_maximum_fusion.1), channel_id=1, source_target_pairs={{0,640},{128,768},{256,896},{384,0},{512,128},{640,256},{768,384},... | collective-permute-start | bytes 497672 | tf_op jit(solution)/shard_map/ppermute | solution.py:52
  186.8 46.2 %all-to-all-start.3 = ((bf16[64,35,128]{2,1,0:T(8,128)(2,1)}), bf16[64,35,128]{2,1,0:T(8,128)(2,1)S(1)}, u32[]{:S(2)}, u32[]{:S(2)}) async-start(bf16[64,35,128]{2,1,0:T(8,128)(2,1)} %reshape.82), calls=%async_computation.3 | async-start | bytes 1310720 | tf_op jit(solution)/shard_map/all_to_all | solution.py:46
  202.4 14.4 %collective-permute-start.12 = (bf16[648,128]{1,0:T(8,128)(2,1)S(1)}, bf16[648,128]{1,0:T(8,128)(2,1)S(1)}, u32[]{:S(2)}, u32[]{:S(2)}) collective-permute-start(bf16[648,128]{1,0:T(8,128)(2,1)S(1)} %pad_maximum_fusion.1), channel_id=1, source_target_pairs={{0,384},{128,512},{256,640},{384,768},{512,896},{640,0},{768,128},... | collective-permute-start | bytes 497672 | tf_op jit(solution)/shard_map/ppermute | solution.py:52
  206.7 15.3 %collective-permute-start.13 = (bf16[648,128]{1,0:T(8,128)(2,1)S(1)}, bf16[648,128]{1,0:T(8,128)(2,1)S(1)}, u32[]{:S(2)}, u32[]{:S(2)}) collective-permute-start(bf16[648,128]{1,0:T(8,128)(2,1)S(1)} %pad_maximum_fusion.1), channel_id=1, source_target_pairs={{0,512},{128,640},{256,768},{384,896},{512,0},{640,128},{768,256},... | collective-permute-start | bytes 497672 | tf_op jit(solution)/shard_map/ppermute | solution.py:52
  222.0 1.1 copy-start.5
  223.6 2.7 copy-start.3
  233.1 0.8 copy-start.1
  233.9 45.7 %all-to-all-start.4 = ((bf16[64,36,128]{2,1,0:T(8,128)(2,1)}), bf16[64,36,128]{2,1,0:T(8,128)(2,1)S(1)}, u32[]{:S(2)}, u32[]{:S(2)}) async-start(bf16[64,36,128]{2,1,0:T(8,128)(2,1)} %pad_maximum_fusion), calls=%async_computation.4 | async-start | bytes 1310720 | tf_op jit(solution)/shard_map/all_to_all | solution.py:46

commit v3 on v2

v3 whole, which is shorter than its diff:
```python
import jax
import jax.numpy as jnp
from jax import lax
from jax.sharding import Mesh
from jax.sharding import PartitionSpec as P


LANES = 128
ALONG_X = 4
F32 = jnp.float32
BF16 = jnp.bfloat16


def matmul(a, b):
    return jnp.dot(a, b, preferred_element_type=F32)


def experts(tokens, routes, event_weights, cotangent, w_gate, w_up, w_down):
    along_z, along_x = lax.axis_size("z"), lax.axis_size("x")
    owners = along_z * along_x
    parts = lax.axis_size("ctx")
    rows, fanout = routes.shape
    _, columns, hidden = w_gate.shape
    capacity = max(2, 5 * rows * fanout // (4 * owners))
    slots = owners * capacity
    piece = hidden // parts
    column = along_z * capacity
    tiles = along_x * capacity * columns // LANES

    flat = routes.reshape(-1)
    named = (flat[:, None] == jnp.arange(owners, dtype=jnp.int32)[None, :]).astype(BF16)
    events = rows * fanout
    earlier = (
        jnp.arange(events)[:, None] > jnp.arange(events)[None, :]
    ).astype(BF16)
    before = matmul(earlier, named)
    places = jnp.sum(before * named.astype(F32), axis=1).astype(jnp.int32)
    steps_x = lax.rem(lax.rem(flat, along_x) - lax.axis_index("x") + along_x, along_x)
    targets = (steps_x * column + flat // along_x * capacity + places).reshape(rows, fanout)
    from_z = (flat // along_x).reshape(rows, fanout)
    from_lane = (steps_x * capacity + places).reshape(rows, fanout)
    slot_ids = jnp.arange(slots, dtype=jnp.int32)
    picks = [slot_ids[:, None] == targets[:, k][None, :] for k in range(fanout)]
    pick_any = sum(p.astype(BF16) for p in picks)
    slot_weights = sum(
        jnp.sum(jnp.where(p, event_weights[:, k][None, :], 0.0), axis=1)
        for k, p in enumerate(picks)
    )

    me = lax.axis_index("ctx")

    def along(value, step):
        return lax.ppermute(value, "x", [(i, (i + step) % along_x) for i in range(along_x)])

    def exchange(buffer):
        return lax.all_to_all(buffer, "z", split_axis=0, concat_axis=0, tiled=True)

    by_z = jnp.arange(slots, dtype=jnp.int32)
    wide = along_x * capacity
    by_z = by_z % wide // capacity * column + by_z // wide * capacity + by_z % capacity
    reorder = (by_z[:, None] == slot_ids[None, :]).astype(BF16)

    def to_columns(value):
        pieces = [value[step * column : (step + 1) * column] for step in range(along_x)]
        pieces = [pieces[0]] + [along(pieces[step], step) for step in range(1, along_x)]
        pieces = matmul(reorder, jnp.concatenate(pieces, axis=0)).astype(BF16)
        return pieces.reshape(along_z, tiles, LANES)

    def from_columns(value, tail=None):
        value = matmul(reorder.T, value.reshape(slots, columns)).astype(BF16)
        pieces = [value[step * column : (step + 1) * column] for step in range(along_x)]
        if tail is not None:
            pieces = [jnp.concatenate([piece, tail], axis=0) for piece in pieces]
        return [pieces[0]] + [along(pieces[step], -step) for step in range(1, along_x)]

    def block(value, step):
        return lax.squeeze(lax.dynamic_slice_in_dim(value, lax.rem(me + step, parts), 1, 0), (0,))

    def shifted(value, step):
        return lax.ppermute(value, "ctx", [(i, (i + step) % parts) for i in range(parts)])

    steps = sorted(range(1, parts), key=lambda step: (min(step, parts - step), step))

    send_tokens = to_columns(matmul(pick_any, tokens).astype(BF16))
    recv_tokens = exchange(send_tokens)
    send_cots = to_columns((slot_weights[:, None] * matmul(pick_any, cotangent)).astype(BF16))
    gate_w = w_gate[0].reshape(columns, parts, piece).transpose(1, 0, 2)
    up_w = w_up[0].reshape(columns, parts, piece).transpose(1, 0, 2)
    recv_tokens, send_cots, gate_w, up_w = lax.optimization_barrier(
        (recv_tokens, send_cots, gate_w, up_w)
    )
    recv_cots = exchange(send_cots)
    expert_in = recv_tokens.reshape(slots, columns)
    expert_cot = recv_cots.reshape(slots, columns)

    down_w = w_down[0].reshape(parts, piece, columns)

    gate_up = jnp.concatenate(
        [
            jnp.einsum("sd,ydj->ysj", expert_in, gate_w, preferred_element_type=F32).astype(BF16),
            jnp.einsum("sd,ydj->ysj", expert_in, up_w, preferred_element_type=F32).astype(BF16),
        ],
        axis=1,
    )
    arrived = [shifted(block(gate_up, step), step) for step in steps]
    gate_up = sum((a.astype(F32) for a in arrived), block(gate_up, 0).astype(F32))
    gate_pre, up_pre = gate_up[:slots], gate_up[slots:]
    squash = jax.nn.sigmoid(gate_pre)
    hidden_act = (gate_pre * squash * up_pre).astype(BF16)

    back = jnp.einsum("sd,yjd->ysj", expert_cot, down_w, preferred_element_type=F32).astype(BF16)
    mixed_rows = jnp.concatenate([back, jnp.broadcast_to(hidden_act, back.shape)], axis=1)
    mixed_rows = lax.all_to_all(mixed_rows, "ctx", split_axis=0, concat_axis=0, tiled=True)
    back, hidden_all = mixed_rows[:, :slots], mixed_rows[:, slots:]
    expert_out = jnp.einsum("ysj,yjd->sd", hidden_all, down_w, preferred_element_type=F32).astype(BF16)
    back_out = exchange(expert_out.reshape(along_z, tiles, LANES))

    back_pre = jnp.sum(back.astype(F32), axis=0)
    grad_gate = (back_pre * up_pre * squash * (1.0 + gate_pre * (1.0 - squash))).astype(BF16)
    grad_up = (back_pre * gate_pre * squash).astype(BF16)
    inner = jnp.sum(hidden_act.astype(F32) * back_pre, axis=1)
    high = lax.reduce_precision(inner, 8, 7)
    inner_rows = jnp.stack([high, inner - high], axis=0).astype(BF16)
    inner_rows = jnp.pad(inner_rows.reshape(-1), (0, 8 * LANES - 2 * slots)).reshape(8, LANES)
    grads = jnp.concatenate([grad_gate, grad_up, inner_rows], axis=0)
    arrived = [shifted(grads, -step) for step in steps]
    gathered = jnp.zeros((parts, *grads.shape), BF16)
    for step, value in zip([0, *steps], [grads, *arrived]):
        gathered = lax.dynamic_update_slice(gathered, value[None], (lax.rem(me + step, parts), 0, 0))
    grads = gathered
    inner = jnp.sum(grads[:, 2 * slots :, :].reshape(parts, -1).astype(F32), axis=0)
    inner = inner[:slots] + inner[slots : 2 * slots]
    event_grad = (
        jnp.einsum("ysj,ydj->sd", grads[:, :slots], gate_w, preferred_element_type=F32)
        + jnp.einsum("ysj,ydj->sd", grads[:, slots : 2 * slots], up_w, preferred_element_type=F32)
    ).astype(BF16)
    high = lax.reduce_precision(inner, 8, 7)
    extra = jnp.concatenate(
        [high.reshape(along_z, -1), (inner - high).reshape(along_z, -1)], axis=1
    ).astype(BF16)
    extra = jnp.pad(extra, ((0, 0), (0, LANES - 2 * wide)))[:, None, :]
    back_grad = exchange(
        jnp.concatenate([event_grad.reshape(along_z, tiles, LANES), extra], axis=1)
    )
    back_out = jnp.concatenate(from_columns(back_out), axis=0)
    tail = jnp.pad(back_grad[:, tiles], ((0, 0), (0, columns - LANES)))
    pieces = from_columns(back_grad[:, :tiles], tail)
    back_grad = jnp.concatenate([piece[:column] for piece in pieces], axis=0)
    lane = jnp.arange(LANES, dtype=jnp.int32)[None, :]
    inner = sum(
        jnp.where(lane % wide // capacity == step, piece[column:, :LANES], 0)
        for step, piece in enumerate(pieces)
    )

    mixed = sum(
        event_weights[:, k][:, None] * matmul(p.astype(BF16).T, back_out) for k, p in enumerate(picks)
    ).astype(BF16)
    token_grad = matmul(pick_any.T, back_grad).astype(BF16)
    z_ids = jnp.arange(along_z, dtype=jnp.int32)[None, :]
    weight_grad = []
    for k in range(fanout):
        values = matmul((from_z[:, k][:, None] == z_ids).astype(BF16), inner)
        held = (lane < 2 * wide) & (lane % wide == from_lane[:, k][:, None])
        weight_grad.append(jnp.sum(jnp.where(held, values, 0.0), axis=1))
    weight_grad = jnp.stack(weight_grad, axis=1) / event_weights
    return (mixed, token_grad, weight_grad)


def solution(mesh):
    parts, owners, reps = mesh.devices.shape
    chips = mesh.devices.reshape(parts, owners // ALONG_X, ALONG_X, reps)
    grid = Mesh(chips, ("ctx", "z", "x", "rep"))
    rows = P(("rep", "z", "x"), "ctx")
    pairs = P(("rep", "z", "x"), None)
    in_specs = (
        rows,
        pairs,
        pairs,
        P(("z", "x"), "ctx"),
        P(("z", "x"), "ctx", None),
        P(("z", "x"), "ctx", None),
        P(("z", "x"), None, "ctx"),
    )
    return jax.shard_map(experts, mesh=grid, in_specs=in_specs, out_specs=(rows, rows, pairs), check_vma=False)
```

time: 283 us -> 298 us (1.053)
  the two profiles are of different devices: /device:TPU:2 before, /device:TPU:80 now
where the time goes in v3:
time: 298 us; the launch traced here: 296 us
  starting transfers between devices  159 us (53%)
  waiting for transfers between devices  47.2 us (16%)
  blocking collectives  35 us (12%)
  local copies, waits for them, and re-layouts  25.6 us (9%)
  matrix products  18.4 us (6%)
  other arithmetic  9.15 us (3%)
    ppermute x14, starting transfers between devices, shifted(): lax.ppermute(value, 'ctx', [(i, (i + step) % parts) for i in range(parts)])  55.1 us
    ppermute x12, starting transfers between devices, along(): lax.ppermute(value, 'x', [(i, (i + step) % along_x) for i in range(along_...  54.6 us
    all_to_all x4, starting transfers between devices, exchange(): return lax.all_to_all(buffer, 'z', split_axis=0, concat_axis=0, tiled=True)  49.3 us
    all_to_all x1, blocking collectives, experts(): lax.all_to_all(mixed_rows, 'ctx', split_axis=0, concat_axis=0, tiled=True)  35 us
    ppermute x14, waiting for transfers between devices, shifted(): lax.ppermute(value, 'ctx', [(i, (i + step) % parts) for i in range(parts)])  19.3 us
    ppermute x12, waiting for transfers between devices, along(): lax.ppermute(value, 'x', [(i, (i + step) % along_x) for i in range(along_...  15.1 us
    all_to_all x4, waiting for transfers between devices, exchange(): return lax.all_to_all(buffer, 'z', split_axis=0, concat_axis=0, tiled=True)  12.8 us
    dot_general x12, matrix products, matmul(): return jnp.dot(a, b, preferred_element_type=F32)  8.91 us
  transfers between devices with their start and end apart: 30, of which 10 were waited for; matrix products, arithmetic and copies ran while one was open for 12% of the time, Pallas kernels for 0%

profile of v3, /device:TPU:80, one launch (start us, length us, event | category | flops | bytes accessed | tf_op | source)
XLA Modules:
  0.0 296.0 jit_solution(8568983376760670117)
XLA Ops:
  5.1 3.4 %collective-permute-start = (bf16[80,896]{1,0:T(8,128)(2,1)S(1)}, bf16[80,896]{1,0:T(8,128)(2,1)S(1)}, u32[]{:S(2)}, u32[]{:S(2)}) collective-permute-start(bf16[80,896]{1,0:T(8,128)(2,1)S(1)} %get-tuple-element.38), channel_id=1, source_target_pairs={{0,2},{2,4},{4,6},{6,0},{1,3},{3,5},{5,7},{7,1},{8,10},{10,12},{12... | collective-permute-start | bytes 430088 | tf_op jit(solution)/shard_map/ppermute | solution.py:53
  8.5 4.6 %collective-permute-start.1 = (bf16[80,896]{1,0:T(8,128)(2,1)S(1)}, bf16[80,896]{1,0:T(8,128)(2,1)S(1)}, u32[]{:S(2)}, u32[]{:S(2)}) collective-permute-start(bf16[80,896]{1,0:T(8,128)(2,1)S(1)} %get-tuple-element.37), channel_id=1, source_target_pairs={{0,4},{2,6},{4,0},{6,2},{1,5},{3,7},{5,1},{7,3},{8,12},{10,14},{12... | collective-permute-start | bytes 430088 | tf_op jit(solution)/shard_map/ppermute | solution.py:53
  13.2 3.3 %collective-permute-start.2 = (bf16[80,896]{1,0:T(8,128)(2,1)S(1)}, bf16[80,896]{1,0:T(8,128)(2,1)S(1)}, u32[]{:S(2)}, u32[]{:S(2)}) collective-permute-start(bf16[80,896]{1,0:T(8,128)(2,1)S(1)} %get-tuple-element.36), channel_id=1, source_target_pairs={{0,6},{2,0},{4,2},{6,4},{1,7},{3,1},{5,3},{7,5},{8,14},{10,8},{12,... | collective-permute-start | bytes 430088 | tf_op jit(solution)/shard_map/ppermute | solution.py:53
  22.1 18.4 %all-to-all-start = ((bf16[16,140,128]{2,1,0:T(8,128)(2,1)}), bf16[16,140,128]{2,1,0:T(8,128)(2,1)S(1)}, u32[]{:S(2)}, u32[]{:S(2)}) async-start(bf16[16,140,128]{2,1,0:T(8,128)(2,1)} %reshape.162), calls=%async_computation | async-start | bytes 1179648 | tf_op jit(solution)/shard_map/all_to_all | solution.py:56
  41.2 3.4 %collective-permute-start.3 = (bf16[80,896]{1,0:T(8,128)(2,1)S(1)}, bf16[80,896]{1,0:T(8,128)(2,1)S(1)}, u32[]{:S(2)}, u32[]{:S(2)}) collective-permute-start(bf16[80,896]{1,0:T(8,128)(2,1)S(1)} %get-tuple-element.34), channel_id=1, source_target_pairs={{0,2},{2,4},{4,6},{6,0},{1,3},{3,5},{5,7},{7,1},{8,10},{10,12},{12... | collective-permute-start | bytes 430088 | tf_op jit(solution)/shard_map/ppermute | solution.py:53
  44.7 4.5 %collective-permute-start.4 = (bf16[80,896]{1,0:T(8,128)(2,1)S(1)}, bf16[80,896]{1,0:T(8,128)(2,1)S(1)}, u32[]{:S(2)}, u32[]{:S(2)}) collective-permute-start(bf16[80,896]{1,0:T(8,128)(2,1)S(1)} %get-tuple-element.33), channel_id=1, source_target_pairs={{0,4},{2,6},{4,0},{6,2},{1,5},{3,7},{5,1},{7,3},{8,12},{10,14},{12... | collective-permute-start | bytes 430088 | tf_op jit(solution)/shard_map/ppermute | solution.py:53
  49.1 2.6 collective-permute-start.5
  58.2 12.2 %all-to-all-done = bf16[16,140,128]{2,1,0:T(8,128)(2,1)S(1)} async-done(((bf16[16,140,128]{2,1,0:T(8,128)(2,1)}), bf16[16,140,128]{2,1,0:T(8,128)(2,1)S(1)}, u32[]{:S(2)}, u32[]{:S(2)}) %all-to-all-start) | async-done | bytes 573472 | tf_op jit(solution)/shard_map/all_to_all | solution.py:56
  70.4 6.7 %all-to-all-start.1 = ((bf16[16,140,128]{2,1,0:T(8,128)(2,1)}), bf16[16,140,128]{2,1,0:T(8,128)(2,1)}, u32[]{:S(2)}, u32[]{:S(2)}) async-start(bf16[16,140,128]{2,1,0:T(8,128)(2,1)} %reshape.163), calls=%async_computation.1 | async-start | bytes 1179648 | tf_op jit(solution)/shard_map/all_to_all | solution.py:56
  78.5 2.5 fusion.5
  83.9 5.8 %collective-permute-start.10 = (bf16[640,128]{1,0:T(8,128)(2,1)}, bf16[640,128]{1,0:T(8,128)(2,1)S(1)}, u32[]{:S(2)}, u32[]{:S(2)}) collective-permute-start(bf16[640,128]{1,0:T(8,128)(2,1)} %get-tuple-element.21), channel_id=1, source_target_pairs={{0,384},{128,512},{256,640},{384,768},{512,896},{640,0},{768,128},... | collective-permute-start | bytes 491528 | tf_op jit(solution)/shard_map/ppermute | solution.py:80
  89.7 3.0 %collective-permute-start.11 = (bf16[640,128]{1,0:T(8,128)(2,1)}, bf16[640,128]{1,0:T(8,128)(2,1)S(1)}, u32[]{:S(2)}, u32[]{:S(2)}) collective-permute-start(bf16[640,128]{1,0:T(8,128)(2,1)} %get-tuple-element.22), channel_id=1, source_target_pairs={{0,640},{128,768},{256,896},{384,0},{512,128},{640,256},{768,384},... | collective-permute-start | bytes 491528 | tf_op jit(solution)/shard_map/ppermute | solution.py:80
  95.0 3.6 %collective-permute-start.7 = (bf16[640,128]{1,0:T(8,128)(2,1)}, bf16[640,128]{1,0:T(8,128)(2,1)}, u32[]{:S(2)}, u32[]{:S(2)}) collective-permute-start(bf16[640,128]{1,0:T(8,128)(2,1)} %get-tuple-element.18), channel_id=1, source_target_pairs={{0,896},{128,0},{256,128},{384,256},{512,384},{640,512},{768,640},... | collective-permute-start | bytes 491528 | tf_op jit(solution)/shard_map/ppermute | solution.py:80
  98.6 6.9 %collective-permute-start.8 = (bf16[640,128]{1,0:T(8,128)(2,1)}, bf16[640,128]{1,0:T(8,128)(2,1)}, u32[]{:S(2)}, u32[]{:S(2)}) collective-permute-start(bf16[640,128]{1,0:T(8,128)(2,1)} %get-tuple-element.19), channel_id=1, source_target_pairs={{0,256},{128,384},{256,512},{384,640},{512,768},{640,896},{768,0},... | collective-permute-start | bytes 491528 | tf_op jit(solution)/shard_map/ppermute | solution.py:80
  108.2 4.3 %collective-permute-start.12 = (bf16[640,128]{1,0:T(8,128)(2,1)}, bf16[640,128]{1,0:T(8,128)(2,1)}, u32[]{:S(2)}, u32[]{:S(2)}) collective-permute-start(bf16[640,128]{1,0:T(8,128)(2,1)} %fusion.66), channel_id=1, source_target_pairs={{0,512},{128,640},{256,768},{384,896},{512,0},{640,128},{768,256},... | collective-permute-start | bytes 491528 | tf_op jit(solution)/shard_map/ppermute | solution.py:80
  112.5 11.6 %collective-permute-done.9 = bf16[640,128]{1,0:T(8,128)(2,1)} collective-permute-done((bf16[640,128]{1,0:T(8,128)(2,1)}, bf16[640,128]{1,0:T(8,128)(2,1)}, u32[]{:S(2)}, u32[]{:S(2)}) %collective-permute-start.9) | collective-permute-done | bytes 163872 | tf_op jit(solution)/shard_map/ppermute | solution.py:80
  128.5 35.0 %all_to_all.25 = bf16[8,640,128]{2,1,0:T(8,128)(2,1)S(1)} all-to-all(bf16[8,640,128]{2,1,0:T(8,128)(2,1)S(1)} %pad_maximum_fusion), channel_id=1, replica_groups=mesh['ctx'=8,'z'=16,'x'=4,'rep'=2] {'ctx'}, dimensions={0} | all-to-all | bytes 2621440 | tf_op jit(solution)/shard_map/all_to_all | solution.py:113
  165.4 3.7 %collective-permute-start.16 = (bf16[648,128]{1,0:T(8,128)(2,1)S(1)}, bf16[648,128]{1,0:T(8,128)(2,1)}, u32[]{:S(2)}, u32[]{:S(2)}) collective-permute-start(bf16[648,128]{1,0:T(8,128)(2,1)S(1)} %pad_maximum_fusion.3), channel_id=1, source_target_pairs={{0,896},{128,0},{256,128},{384,256},{512,384},{640,512},{768,640},... | collective-permute-start | bytes 497672 | tf_op jit(solution)/shard_map/ppermute | solution.py:80
  171.2 4.6 %collective-permute-start.18 = (bf16[648,128]{1,0:T(8,128)(2,1)S(1)}, bf16[648,128]{1,0:T(8,128)(2,1)}, u32[]{:S(2)}, u32[]{:S(2)}) collective-permute-start(bf16[648,128]{1,0:T(8,128)(2,1)S(1)} %pad_maximum_fusion.3), channel_id=1, source_target_pairs={{0,768},{128,896},{256,0},{384,128},{512,256},{640,384},{768,512},... | collective-permute-start | bytes 497672 | tf_op jit(solution)/shard_map/ppermute | solution.py:80
  175.9 3.3 %collective-permute-start.19 = (bf16[648,128]{1,0:T(8,128)(2,1)S(1)}, bf16[648,128]{1,0:T(8,128)(2,1)}, u32[]{:S(2)}, u32[]{:S(2)}) collective-permute-start(bf16[648,128]{1,0:T(8,128)(2,1)S(1)} %pad_maximum_fusion.3), channel_id=1, source_target_pairs={{0,256},{128,384},{256,512},{384,640},{512,768},{640,896},{768,0},... | collective-permute-start | bytes 497672 | tf_op jit(solution)/shard_map/ppermute | solution.py:80
  179.2 5.5 %collective-permute-start.20 = (bf16[648,128]{1,0:T(8,128)(2,1)S(1)}, bf16[648,128]{1,0:T(8,128)(2,1)}, u32[]{:S(2)}, u32[]{:S(2)}) collective-permute-start(bf16[648,128]{1,0:T(8,128)(2,1)S(1)} %pad_maximum_fusion.3), channel_id=1, source_target_pairs={{0,640},{128,768},{256,896},{384,0},{512,128},{640,256},{768,384},... | collective-permute-start | bytes 497672 | tf_op jit(solution)/shard_map/ppermute | solution.py:80
  188.8 12.2 %all-to-all-start.3 = ((bf16[16,140,128]{2,1,0:T(8,128)(2,1)}), bf16[16,140,128]{2,1,0:T(8,128)(2,1)S(1)}, u32[]{:S(2)}, u32[]{:S(2)}) async-start(bf16[16,140,128]{2,1,0:T(8,128)(2,1)} %reshape.166), calls=%async_computation.3 | async-start | bytes 1179648 | tf_op jit(solution)/shard_map/all_to_all | solution.py:56
  201.2 3.7 %collective-permute-start.21 = (bf16[648,128]{1,0:T(8,128)(2,1)S(1)}, bf16[648,128]{1,0:T(8,128)(2,1)S(1)}, u32[]{:S(2)}, u32[]{:S(2)}) collective-permute-start(bf16[648,128]{1,0:T(8,128)(2,1)S(1)} %pad_maximum_fusion.3), channel_id=1, source_target_pairs={{0,384},{128,512},{256,640},{384,768},{512,896},{640,0},{768,128},... | collective-permute-start | bytes 497672 | tf_op jit(solution)/shard_map/ppermute | solution.py:80
  205.9 4.4 %collective-permute-start.22 = (bf16[648,128]{1,0:T(8,128)(2,1)S(1)}, bf16[648,128]{1,0:T(8,128)(2,1)S(1)}, u32[]{:S(2)}, u32[]{:S(2)}) collective-permute-start(bf16[648,128]{1,0:T(8,128)(2,1)S(1)} %pad_maximum_fusion.3), channel_id=1, source_target_pairs={{0,512},{128,640},{256,768},{384,896},{512,0},{640,128},{768,256},... | collective-permute-start | bytes 497672 | tf_op jit(solution)/shard_map/ppermute | solution.py:80
  214.1 7.6 %collective-permute-done.21 = bf16[648,128]{1,0:T(8,128)(2,1)S(1)} collective-permute-done((bf16[648,128]{1,0:T(8,128)(2,1)S(1)}, bf16[648,128]{1,0:T(8,128)(2,1)S(1)}, u32[]{:S(2)}, u32[]{:S(2)}) %collective-permute-start.21) | collective-permute-done | bytes 165920 | tf_op jit(solution)/shard_map/ppermute | solution.py:80
  228.9 12.0 %all-to-all-start.4 = ((bf16[16,141,128]{2,1,0:T(8,128)(2,1)}), bf16[16,141,128]{2,1,0:T(8,128)(2,1)S(1)}, u32[]{:S(2)}, u32[]{:S(2)}) async-start(bf16[16,141,128]{2,1,0:T(8,128)(2,1)} %pad_maximum_fusion.1), calls=%async_computation.4 | async-start | bytes 1179648 | tf_op jit(solution)/shard_map/all_to_all | solution.py:56
  244.3 4.6 %collective-permute-start.13 = (bf16[80,896]{1,0:T(8,128)(2,1)S(1)}, bf16[80,896]{1,0:T(8,128)(2,1)S(1)}, u32[]{:S(2)}, u32[]{:S(2)}) collective-permute-start(bf16[80,896]{1,0:T(8,128)(2,1)S(1)} %get-tuple-element.30), channel_id=1, source_target_pairs={{0,6},{2,0},{4,2},{6,4},{1,7},{3,1},{5,3},{7,5},{8,14},{10,8},{12,... | collective-permute-start | bytes 430088 | tf_op jit(solution)/shard_map/ppermute | solution.py:53
  248.9 7.7 %collective-permute-start.14 = (bf16[80,896]{1,0:T(8,128)(2,1)S(1)}, bf16[80,896]{1,0:T(8,128)(2,1)S(1)}, u32[]{:S(2)}, u32[]{:S(2)}) collective-permute-start(bf16[80,896]{1,0:T(8,128)(2,1)S(1)} %get-tuple-element.29), channel_id=1, source_target_pairs={{0,4},{2,6},{4,0},{6,2},{1,5},{3,7},{5,1},{7,3},{8,12},{10,14},{12... | collective-permute-start | bytes 430088 | tf_op jit(solution)/shard_map/ppermute | solution.py:53
  260.0 4.7 %collective-permute-done.15 = bf16[80,896]{1,0:T(8,128)(2,1)S(1)} collective-permute-done((bf16[80,896]{1,0:T(8,128)(2,1)S(1)}, bf16[80,896]{1,0:T(8,128)(2,1)S(1)}, u32[]{:S(2)}, u32[]{:S(2)}) %collective-permute-start.15) | collective-permute-done | bytes 143392 | tf_op jit(solution)/shard_map/ppermute | solution.py:53
  268.7 4.6 %collective-permute-start.23 = (bf16[96,896]{1,0:T(8,128)(2,1)S(1)}, bf16[96,896]{1,0:T(8,128)(2,1)S(1)}, u32[]{:S(2)}, u32[]{:S(2)}) collective-permute-start(bf16[96,896]{1,0:T(8,128)(2,1)S(1)} %get-tuple-element.47), channel_id=1, source_target_pairs={{0,6},{2,0},{4,2},{6,4},{1,7},{3,1},{5,3},{7,5},{8,14},{10,8},{12,... | collective-permute-start | bytes 516104 | tf_op jit(solution)/shard_map/ppermute | solution.py:53
  273.2 12.1 %collective-permute-start.24 = (bf16[96,896]{1,0:T(8,128)(2,1)S(1)}, bf16[96,896]{1,0:T(8,128)(2,1)S(1)}, u32[]{:S(2)}, u32[]{:S(2)}) collective-permute-start(bf16[96,896]{1,0:T(8,128)(2,1)S(1)} %get-tuple-element.48), channel_id=1, source_target_pairs={{0,4},{2,6},{4,0},{6,2},{1,5},{3,7},{5,1},{7,3},{8,12},{10,14},{12... | collective-permute-start | bytes 516104 | tf_op jit(solution)/shard_map/ppermute | solution.py:53
  288.7 5.2 %collective-permute-done.25 = bf16[96,896]{1,0:T(8,128)(2,1)S(1)} collective-permute-done((bf16[96,896]{1,0:T(8,128)(2,1)S(1)}, bf16[96,896]{1,0:T(8,128)(2,1)S(1)}, u32[]{:S(2)}, u32[]{:S(2)}) %collective-permute-start.25) | collective-permute-done | bytes 172064 | tf_op jit(solution)/shard_map/ppermute | solution.py:53
  (174 shorter events, 66.7 us)
Async XLA Ops:
  0.6 126.8 %copy-start = (bf16[1,1024,896]{2,1,0:T(8,128)(2,1)S(1)}, bf16[1,1024,896]{2,1,0:T(8,128)(2,1)}, u32[]{:S(2)}) copy-start(bf16[1,1024,896]{2,1,0:T(8,128)(2,1)} %param.13) | copy-start | bytes 5505028
  5.1 11.4 %collective-permute-start = (bf16[80,896]{1,0:T(8,128)(2,1)S(1)}, bf16[80,896]{1,0:T(8,128)(2,1)S(1)}, u32[]{:S(2)}, u32[]{:S(2)}) collective-permute-start(bf16[80,896]{1,0:T(8,128)(2,1)S(1)} %get-tuple-element.38), channel_id=1, source_target_pairs={{0,2},{2,4},{4,6},{6,0},{1,3},{3,5},{5,7},{7,1},{8,10},{10,12},{12... | collective-permute-start | bytes 430088 | tf_op jit(solution)/shard_map/ppermute | solution.py:53
  8.5 9.3 %collective-permute-start.1 = (bf16[80,896]{1,0:T(8,128)(2,1)S(1)}, bf16[80,896]{1,0:T(8,128)(2,1)S(1)}, u32[]{:S(2)}, u32[]{:S(2)}) collective-permute-start(bf16[80,896]{1,0:T(8,128)(2,1)S(1)} %get-tuple-element.37), channel_id=1, source_target_pairs={{0,4},{2,6},{4,0},{6,2},{1,5},{3,7},{5,1},{7,3},{8,12},{10,14},{12... | collective-permute-start | bytes 430088 | tf_op jit(solution)/shard_map/ppermute | solution.py:53
  13.2 7.0 %collective-permute-start.2 = (bf16[80,896]{1,0:T(8,128)(2,1)S(1)}, bf16[80,896]{1,0:T(8,128)(2,1)S(1)}, u32[]{:S(2)}, u32[]{:S(2)}) collective-permute-start(bf16[80,896]{1,0:T(8,128)(2,1)S(1)} %get-tuple-element.36), channel_id=1, source_target_pairs={{0,6},{2,0},{4,2},{6,4},{1,7},{3,1},{5,3},{7,5},{8,14},{10,8},{12,... | collective-permute-start | bytes 430088 | tf_op jit(solution)/shard_map/ppermute | solution.py:53
  16.6 39.7 %copy-start.14 = (s32[320]{0:T(512)}, s32[320]{0:T(512)S(1)}, u32[]{:S(2)}) copy-start(s32[320]{0:T(512)S(1)} %fusion.103) | copy-start | bytes 3844
  22.1 48.2 %all-to-all-start = ((bf16[16,140,128]{2,1,0:T(8,128)(2,1)}), bf16[16,140,128]{2,1,0:T(8,128)(2,1)S(1)}, u32[]{:S(2)}, u32[]{:S(2)}) async-start(bf16[16,140,128]{2,1,0:T(8,128)(2,1)} %reshape.162), calls=%async_computation | async-start | bytes 1179648 | tf_op jit(solution)/shard_map/all_to_all | solution.py:56
  41.2 15.0 %collective-permute-start.3 = (bf16[80,896]{1,0:T(8,128)(2,1)S(1)}, bf16[80,896]{1,0:T(8,128)(2,1)S(1)}, u32[]{:S(2)}, u32[]{:S(2)}) collective-permute-start(bf16[80,896]{1,0:T(8,128)(2,1)S(1)} %get-tuple-element.34), channel_id=1, source_target_pairs={{0,2},{2,4},{4,6},{6,0},{1,3},{3,5},{5,7},{7,1},{8,10},{10,12},{12... | collective-permute-start | bytes 430088 | tf_op jit(solution)/shard_map/ppermute | solution.py:53
  44.7 11.6 %collective-permute-start.4 = (bf16[80,896]{1,0:T(8,128)(2,1)S(1)}, bf16[80,896]{1,0:T(8,128)(2,1)S(1)}, u32[]{:S(2)}, u32[]{:S(2)}) collective-permute-start(bf16[80,896]{1,0:T(8,128)(2,1)S(1)} %get-tuple-element.33), channel_id=1, source_target_pairs={{0,4},{2,6},{4,0},{6,2},{1,5},{3,7},{5,1},{7,3},{8,12},{10,14},{12... | collective-permute-start | bytes 430088 | tf_op jit(solution)/shard_map/ppermute | solution.py:53
  49.1 7.1 %collective-permute-start.5 = (bf16[80,896]{1,0:T(8,128)(2,1)S(1)}, bf16[80,896]{1,0:T(8,128)(2,1)S(1)}, u32[]{:S(2)}, u32[]{:S(2)}) collective-permute-start(bf16[80,896]{1,0:T(8,128)(2,1)S(1)} %get-tuple-element.32), channel_id=1, source_target_pairs={{0,6},{2,0},{4,2},{6,4},{1,7},{3,1},{5,3},{7,5},{8,14},{10,8},{12,... | collective-permute-start | bytes 430088 | tf_op jit(solution)/shard_map/ppermute | solution.py:53
  70.4 55.4 %all-to-all-start.1 = ((bf16[16,140,128]{2,1,0:T(8,128)(2,1)}), bf16[16,140,128]{2,1,0:T(8,128)(2,1)}, u32[]{:S(2)}, u32[]{:S(2)}) async-start(bf16[16,140,128]{2,1,0:T(8,128)(2,1)} %reshape.163), calls=%async_computation.1 | async-start | bytes 1179648 | tf_op jit(solution)/shard_map/all_to_all | solution.py:56
  83.9 22.3 %collective-permute-start.10 = (bf16[640,128]{1,0:T(8,128)(2,1)}, bf16[640,128]{1,0:T(8,128)(2,1)S(1)}, u32[]{:S(2)}, u32[]{:S(2)}) collective-permute-start(bf16[640,128]{1,0:T(8,128)(2,1)} %get-tuple-element.21), channel_id=1, source_target_pairs={{0,384},{128,512},{256,640},{384,768},{512,896},{640,0},{768,128},... | collective-permute-start | bytes 491528 | tf_op jit(solution)/shard_map/ppermute | solution.py:80
  89.7 18.4 %collective-permute-start.11 = (bf16[640,128]{1,0:T(8,128)(2,1)}, bf16[640,128]{1,0:T(8,128)(2,1)S(1)}, u32[]{:S(2)}, u32[]{:S(2)}) collective-permute-start(bf16[640,128]{1,0:T(8,128)(2,1)} %get-tuple-element.22), channel_id=1, source_target_pairs={{0,640},{128,768},{256,896},{384,0},{512,128},{640,256},{768,384},... | collective-permute-start | bytes 491528 | tf_op jit(solution)/shard_map/ppermute | solution.py:80
  92.7 19.7 %collective-permute-start.6 = (bf16[640,128]{1,0:T(8,128)(2,1)}, bf16[640,128]{1,0:T(8,128)(2,1)}, u32[]{:S(2)}, u32[]{:S(2)}) collective-permute-start(bf16[640,128]{1,0:T(8,128)(2,1)} %get-tuple-element.17), channel_id=1, source_target_pairs={{0,128},{128,256},{256,384},{384,512},{512,640},{640,768},{768,896... | collective-permute-start | bytes 491528 | tf_op jit(solution)/shard_map/ppermute | solution.py:80
  95.0 17.4 %collective-permute-start.7 = (bf16[640,128]{1,0:T(8,128)(2,1)}, bf16[640,128]{1,0:T(8,128)(2,1)}, u32[]{:S(2)}, u32[]{:S(2)}) collective-permute-start(bf16[640,128]{1,0:T(8,128)(2,1)} %get-tuple-element.18), channel_id=1, source_target_pairs={{0,896},{128,0},{256,128},{384,256},{512,384},{640,512},{768,640},... | collective-permute-start | bytes 491528 | tf_op jit(solution)/shard_map/ppermute | solution.py:80
  98.6 13.9 %collective-permute-start.8 = (bf16[640,128]{1,0:T(8,128)(2,1)}, bf16[640,128]{1,0:T(8,128)(2,1)}, u32[]{:S(2)}, u32[]{:S(2)}) collective-permute-start(bf16[640,128]{1,0:T(8,128)(2,1)} %get-tuple-element.19), channel_id=1, source_target_pairs={{0,256},{128,384},{256,512},{384,640},{512,768},{640,896},{768,0},... | collective-permute-start | bytes 491528 | tf_op jit(solution)/shard_map/ppermute | solution.py:80
  106.2 17.9 %collective-permute-start.9 = (bf16[640,128]{1,0:T(8,128)(2,1)}, bf16[640,128]{1,0:T(8,128)(2,1)}, u32[]{:S(2)}, u32[]{:S(2)}) collective-permute-start(bf16[640,128]{1,0:T(8,128)(2,1)} %get-tuple-element.20), channel_id=1, source_target_pairs={{0,768},{128,896},{256,0},{384,128},{512,256},{640,384},{768,512},... | collective-permute-start | bytes 491528 | tf_op jit(solution)/shard_map/ppermute | solution.py:80
  108.2 16.0 %collective-permute-start.12 = (bf16[640,128]{1,0:T(8,128)(2,1)}, bf16[640,128]{1,0:T(8,128)(2,1)}, u32[]{:S(2)}, u32[]{:S(2)}) collective-permute-start(bf16[640,128]{1,0:T(8,128)(2,1)} %fusion.66), channel_id=1, source_target_pairs={{0,512},{128,640},{256,768},{384,896},{512,0},{640,128},{768,256},... | collective-permute-start | bytes 491528 | tf_op jit(solution)/shard_map/ppermute | solution.py:80
  165.4 35.8 %collective-permute-start.16 = (bf16[648,128]{1,0:T(8,128)(2,1)S(1)}, bf16[648,128]{1,0:T(8,128)(2,1)}, u32[]{:S(2)}, u32[]{:S(2)}) collective-permute-start(bf16[648,128]{1,0:T(8,128)(2,1)S(1)} %pad_maximum_fusion.3), channel_id=1, source_target_pairs={{0,896},{128,0},{256,128},{384,256},{512,384},{640,512},{768,640},... | collective-permute-start | bytes 497672 | tf_op jit(solution)/shard_map/ppermute | solution.py:80
  169.1 36.8 %collective-permute-start.17 = (bf16[648,128]{1,0:T(8,128)(2,1)S(1)}, bf16[648,128]{1,0:T(8,128)(2,1)}, u32[]{:S(2)}, u32[]{:S(2)}) collective-permute-start(bf16[648,128]{1,0:T(8,128)(2,1)S(1)} %pad_maximum_fusion.3), channel_id=1, source_target_pairs={{0,128},{128,256},{256,384},{384,512},{512,640},{640,768},{768,896... | collective-permute-start | bytes 497672 | tf_op jit(solution)/shard_map/ppermute | solution.py:80
  171.2 40.0 %collective-permute-start.18 = (bf16[648,128]{1,0:T(8,128)(2,1)S(1)}, bf16[648,128]{1,0:T(8,128)(2,1)}, u32[]{:S(2)}, u32[]{:S(2)}) collective-permute-start(bf16[648,128]{1,0:T(8,128)(2,1)S(1)} %pad_maximum_fusion.3), channel_id=1, source_target_pairs={{0,768},{128,896},{256,0},{384,128},{512,256},{640,384},{768,512},... | collective-permute-start | bytes 497672 | tf_op jit(solution)/shard_map/ppermute | solution.py:80
  175.9 36.3 %collective-permute-start.19 = (bf16[648,128]{1,0:T(8,128)(2,1)S(1)}, bf16[648,128]{1,0:T(8,128)(2,1)}, u32[]{:S(2)}, u32[]{:S(2)}) collective-permute-start(bf16[648,128]{1,0:T(8,128)(2,1)S(1)} %pad_maximum_fusion.3), channel_id=1, source_target_pairs={{0,256},{128,384},{256,512},{384,640},{512,768},{640,896},{768,0},... | collective-permute-start | bytes 497672 | tf_op jit(solution)/shard_map/ppermute | solution.py:80
  179.2 33.9 %collective-permute-start.20 = (bf16[648,128]{1,0:T(8,128)(2,1)S(1)}, bf16[648,128]{1,0:T(8,128)(2,1)}, u32[]{:S(2)}, u32[]{:S(2)}) collective-permute-start(bf16[648,128]{1,0:T(8,128)(2,1)S(1)} %pad_maximum_fusion.3), channel_id=1, source_target_pairs={{0,640},{128,768},{256,896},{384,0},{512,128},{640,256},{768,384},... | collective-permute-start | bytes 497672 | tf_op jit(solution)/shard_map/ppermute | solution.py:80
  188.8 40.1 %all-to-all-start.3 = ((bf16[16,140,128]{2,1,0:T(8,128)(2,1)}), bf16[16,140,128]{2,1,0:T(8,128)(2,1)S(1)}, u32[]{:S(2)}, u32[]{:S(2)}) async-start(bf16[16,140,128]{2,1,0:T(8,128)(2,1)} %reshape.166), calls=%async_computation.3 | async-start | bytes 1179648 | tf_op jit(solution)/shard_map/all_to_all | solution.py:56
  201.2 20.5 %collective-permute-start.21 = (bf16[648,128]{1,0:T(8,128)(2,1)S(1)}, bf16[648,128]{1,0:T(8,128)(2,1)S(1)}, u32[]{:S(2)}, u32[]{:S(2)}) collective-permute-start(bf16[648,128]{1,0:T(8,128)(2,1)S(1)} %pad_maximum_fusion.3), channel_id=1, source_target_pairs={{0,384},{128,512},{256,640},{384,768},{512,896},{640,0},{768,128},... | collective-permute-start | bytes 497672 | tf_op jit(solution)/shard_map/ppermute | solution.py:80
  205.9 15.8 %collective-permute-start.22 = (bf16[648,128]{1,0:T(8,128)(2,1)S(1)}, bf16[648,128]{1,0:T(8,128)(2,1)S(1)}, u32[]{:S(2)}, u32[]{:S(2)}) collective-permute-start(bf16[648,128]{1,0:T(8,128)(2,1)S(1)} %pad_maximum_fusion.3), channel_id=1, source_target_pairs={{0,512},{128,640},{256,768},{384,896},{512,0},{640,128},{768,256},... | collective-permute-start | bytes 497672 | tf_op jit(solution)/shard_map/ppermute | solution.py:80
  228.9 38.3 %all-to-all-start.4 = ((bf16[16,141,128]{2,1,0:T(8,128)(2,1)}), bf16[16,141,128]{2,1,0:T(8,128)(2,1)S(1)}, u32[]{:S(2)}, u32[]{:S(2)}) async-start(bf16[16,141,128]{2,1,0:T(8,128)(2,1)} %pad_maximum_fusion.1), calls=%async_computation.4 | async-start | bytes 1179648 | tf_op jit(solution)/shard_map/all_to_all | solution.py:56
  244.3 14.5 %collective-permute-start.13 = (bf16[80,896]{1,0:T(8,128)(2,1)S(1)}, bf16[80,896]{1,0:T(8,128)(2,1)S(1)}, u32[]{:S(2)}, u32[]{:S(2)}) collective-permute-start(bf16[80,896]{1,0:T(8,128)(2,1)S(1)} %get-tuple-element.30), channel_id=1, source_target_pairs={{0,6},{2,0},{4,2},{6,4},{1,7},{3,1},{5,3},{7,5},{8,14},{10,8},{12,... | collective-permute-start | bytes 430088 | tf_op jit(solution)/shard_map/ppermute | solution.py:53
  248.9 11.2 %collective-permute-start.14 = (bf16[80,896]{1,0:T(8,128)(2,1)S(1)}, bf16[80,896]{1,0:T(8,128)(2,1)S(1)}, u32[]{:S(2)}, u32[]{:S(2)}) collective-permute-start(bf16[80,896]{1,0:T(8,128)(2,1)S(1)} %get-tuple-element.29), channel_id=1, source_target_pairs={{0,4},{2,6},{4,0},{6,2},{1,5},{3,7},{5,1},{7,3},{8,12},{10,14},{12... | collective-permute-start | bytes 430088 | tf_op jit(solution)/shard_map/ppermute | solution.py:53
  256.6 8.2 %collective-permute-start.15 = (bf16[80,896]{1,0:T(8,128)(2,1)S(1)}, bf16[80,896]{1,0:T(8,128)(2,1)S(1)}, u32[]{:S(2)}, u32[]{:S(2)}) collective-permute-start(bf16[80,896]{1,0:T(8,128)(2,1)S(1)} %get-tuple-element.28), channel_id=1, source_target_pairs={{0,2},{2,4},{4,6},{6,0},{1,3},{3,5},{5,7},{7,1},{8,10},{10,12},{12... | collective-permute-start | bytes 430088 | tf_op jit(solution)/shard_map/ppermute | solution.py:53
  268.7 19.7 %collective-permute-start.23 = (bf16[96,896]{1,0:T(8,128)(2,1)S(1)}, bf16[96,896]{1,0:T(8,128)(2,1)S(1)}, u32[]{:S(2)}, u32[]{:S(2)}) collective-permute-start(bf16[96,896]{1,0:T(8,128)(2,1)S(1)} %get-tuple-element.47), channel_id=1, source_target_pairs={{0,6},{2,0},{4,2},{6,4},{1,7},{3,1},{5,3},{7,5},{8,14},{10,8},{12,... | collective-permute-start | bytes 516104 | tf_op jit(solution)/shard_map/ppermute | solution.py:53
  273.2 15.4 %collective-permute-start.24 = (bf16[96,896]{1,0:T(8,128)(2,1)S(1)}, bf16[96,896]{1,0:T(8,128)(2,1)S(1)}, u32[]{:S(2)}, u32[]{:S(2)}) collective-permute-start(bf16[96,896]{1,0:T(8,128)(2,1)S(1)} %get-tuple-element.48), channel_id=1, source_target_pairs={{0,4},{2,6},{4,0},{6,2},{1,5},{3,7},{5,1},{7,3},{8,12},{10,14},{12... | collective-permute-start | bytes 516104 | tf_op jit(solution)/shard_map/ppermute | solution.py:53
  285.3 8.5 %collective-permute-start.25 = (bf16[96,896]{1,0:T(8,128)(2,1)S(1)}, bf16[96,896]{1,0:T(8,128)(2,1)S(1)}, u32[]{:S(2)}, u32[]{:S(2)}) collective-permute-start(bf16[96,896]{1,0:T(8,128)(2,1)S(1)} %get-tuple-element.49), channel_id=1, source_target_pairs={{0,2},{2,4},{4,6},{6,0},{1,3},{3,5},{5,7},{7,1},{8,10},{10,12},{12... | collective-permute-start | bytes 516104 | tf_op jit(solution)/shard_map/ppermute | solution.py:53
  (27 other events, 399.5 us)

commit v4 on v2

--- a/solution.py
+++ b/solution.py
@@ -2,7 +2,6 @@
 import jax.numpy as jnp
 from jax import lax
 from jax.sharding import PartitionSpec as P
-
 
 LANES = 128
 F32 = jnp.float32
@@ -13,7 +12,7 @@
     return jnp.dot(a, b, preferred_element_type=F32)
 
 
-def experts(tokens, routes, event_weights, cotangent, w_gate, w_up, w_down):
+def shards(tokens, routes, event_weights, cotangent, w_gate, w_up, w_down):
     owners = lax.axis_size("exp")
     parts = lax.axis_size("ctx")
     rows, fanout = routes.shape
@@ -40,21 +39,12 @@
         for k, p in enumerate(picks)
     )
 
-    me = lax.axis_index("ctx")
-
     def send(buffer):
         return lax.all_to_all(buffer, "exp", split_axis=0, concat_axis=0, tiled=True)
 
-    def block(value, step):
-        return lax.squeeze(lax.dynamic_slice_in_dim(value, lax.rem(me + step, parts), 1, 0), (0,))
-
-    def shifted(value, step):
-        return lax.ppermute(value, "ctx", [(i, (i + step) % parts) for i in range(parts)])
-
-    steps = sorted(range(1, parts), key=lambda step: (min(step, parts - step), step))
-
-    send_tokens = matmul(pick_any, tokens).astype(BF16).reshape(owners, tiles, LANES)
-    recv_tokens = send(send_tokens)
+    with jax.named_scope("send_tokens"):
+        send_tokens = matmul(pick_any, tokens).astype(BF16).reshape(owners, tiles, LANES)
+        recv_tokens = send(send_tokens)
     send_cots = (
         (slot_weights[:, None] * matmul(pick_any, cotangent)).astype(BF16).reshape(owners, tiles, LANES)
     )
@@ -63,7 +53,8 @@
     recv_tokens, send_cots, gate_w, up_w = lax.optimization_barrier(
         (recv_tokens, send_cots, gate_w, up_w)
     )
-    recv_cots = send(send_cots)
+    with jax.named_scope("send_cots"):
+        recv_cots = send(send_cots)
     expert_in = recv_tokens.reshape(slots, columns)
     expert_cot = recv_cots.reshape(slots, columns)
 
@@ -76,19 +67,23 @@
         ],
         axis=1,
     )
-    arrived = [shifted(block(gate_up, step), step) for step in steps]
-    gate_up = sum((a.astype(F32) for a in arrived), block(gate_up, 0).astype(F32))
+    with jax.named_scope("reduce_gate_up"):
+        gate_up = lax.psum_scatter(gate_up, "ctx", scatter_dimension=0, tiled=False).astype(F32)
     gate_pre, up_pre = gate_up[:slots], gate_up[slots:]
     squash = jax.nn.sigmoid(gate_pre)
     hidden_act = (gate_pre * squash * up_pre).astype(BF16)
 
-    back = jnp.einsum("sd,yjd->ysj", expert_cot, down_w, preferred_element_type=F32).astype(BF16)
-    hidden_act, back = lax.optimization_barrier((hidden_act, back))
-    back = lax.all_to_all(back, "ctx", split_axis=0, concat_axis=0, tiled=True)
-    hidden_all = lax.all_gather(hidden_act, "ctx", axis=0, tiled=False)
+    with jax.named_scope("back_product"):
+        back = jnp.einsum("sd,yjd->ysj", expert_cot, down_w, preferred_element_type=F32).astype(BF16)
+    hidden_act, _ = lax.optimization_barrier((hidden_act, back))
+    with jax.named_scope("reduce_back"):
+        back = lax.all_to_all(back, "ctx", split_axis=0, concat_axis=0, tiled=True)
+    with jax.named_scope("gather_hidden"):
+        hidden_all = lax.all_gather(hidden_act, "ctx", axis=0, tiled=False)
     expert_out = jnp.einsum("ysj,yjd->sd", hidden_all, down_w, preferred_element_type=F32).astype(BF16)
     back, send_out = lax.optimization_barrier((back, expert_out.reshape(owners, tiles, LANES)))
-    back_out = send(send_out)
+    with jax.named_scope("send_out"):
+        back_out = send(send_out)
 
     back_pre = jnp.sum(back.astype(F32), axis=0)
     grad_gate = (back_pre * up_pre * squash * (1.0 + gate_pre * (1.0 - squash))).astype(BF16)
@@ -98,11 +93,8 @@
     inner_rows = jnp.stack([high, inner - high], axis=0).astype(BF16)
     inner_rows = jnp.pad(inner_rows.reshape(-1), (0, 8 * LANES - 2 * slots)).reshape(8, LANES)
     grads = jnp.concatenate([grad_gate, grad_up, inner_rows], axis=0)
-    arrived = [shifted(grads, -step) for step in steps]
-    gathered = jnp.zeros((parts, *grads.shape), BF16)
-    for step, value in zip([0, *steps], [grads, *arrived]):
-        gathered = lax.dynamic_update_slice(gathered, value[None], (lax.rem(me + step, parts), 0, 0))
-    grads = gathered
+    with jax.named_scope("gather_grads"):
+        grads = lax.all_gather(grads, "ctx", axis=0, tiled=False)
     inner = jnp.sum(grads[:, 2 * slots :, :].reshape(parts, -1).astype(F32), axis=0)
     inner = inner[:slots] + inner[slots : 2 * slots]
     event_grad = (
@@ -114,7 +106,8 @@
         [high.reshape(owners, capacity), (inner - high).reshape(owners, capacity)], axis=1
     ).astype(BF16)
     extra = jnp.pad(extra, ((0, 0), (0, LANES - 2 * capacity)))[:, None, :]
-    back_grad = send(jnp.concatenate([event_grad.reshape(owners, tiles, LANES), extra], axis=1))
+    with jax.named_scope("send_grad"):
+        back_grad = send(jnp.concatenate([event_grad.reshape(owners, tiles, LANES), extra], axis=1))
     back_out = back_out.reshape(slots, columns)
     extra = back_grad[:, tiles, : 2 * capacity].astype(F32)
     inner = (extra[:, :capacity] + extra[:, capacity:]).reshape(slots)
@@ -142,4 +135,4 @@
         P("exp", None, "ctx"),
     )
     out_specs = (P(("rep", "exp"), "ctx"), P(("rep", "exp"), "ctx"), P(("rep", "exp"), None))
-    return jax.shard_map(experts, mesh=mesh, in_specs=in_specs, out_specs=out_specs, check_vma=False)
+    return jax.shard_map(shards, mesh=mesh, in_specs=in_specs, out_specs=out_specs, check_vma=False)

time: 283 us -> 289 us (1.021)
  waiting for transfers between devices: 76.8 us -> 136 us
  starting transfers between devices: 121 us -> 71 us
  between operations: 1.27 us -> 14.3 us
  blocking collectives: 37.1 us -> 26.5 us
  local copies, waits for them, and re-layouts: 22.7 us -> 18.2 us
    ppermute x14 -> x0, starting transfers between devices: 59.3 us -> none  [shifted(): lax.ppermute(value, 'ctx', [(i, (i + step) % parts) for i in range(parts)])]
    all_to_all x4, waiting for transfers between devices: 61.3 us -> 93.7 us  [send(): lax.all_to_all(buffer, 'exp', split_axis=0, concat_axis=0, tiled=True)]
    all_gather x0 -> x1, waiting for transfers between devices: none -> 31.1 us  [shards(): grads = lax.all_gather(grads, 'ctx', axis=0, tiled=False)]
    ppermute x14 -> x0, waiting for transfers between devices: 15.5 us -> none  [shifted(): lax.ppermute(value, 'ctx', [(i, (i + step) % parts) for i in range(parts)])]
    reduce_scatter x0 -> x1, waiting for transfers between devices: none -> 11.2 us  [shards(): lax.psum_scatter(gate_up, 'ctx', scatter_dimension=0, tiled=False)]
    all_gather x1, blocking collectives: 37.1 us -> 26.5 us  [shards(): hidden_all = lax.all_gather(hidden_act, 'ctx', axis=0, tiled=False)]
    all_to_all x4, starting transfers between devices: 57.5 us -> 63.8 us  [send(): lax.all_to_all(buffer, 'exp', split_axis=0, concat_axis=0, tiled=True)]
    unnamed x23 -> x19, local copies, waits for them, and re-layouts: 6.38 us -> 4.48 us
  transfers between devices with their start and end apart: 19 -> 7, of which waited for: 8 -> 5; matrix products, arithmetic and copies ran while one was open for 11% -> 11% of each run, Pallas kernels for 0% -> 0%
where the time goes in v4:
time: 289 us; the launch traced here: 288 us
  waiting for transfers between devices  136 us (47%)
  starting transfers between devices  71 us (25%)
  blocking collectives  26.5 us (9%)
  local copies, waits for them, and re-layouts  18.2 us (6%)
  matrix products  15.7 us (5%)
  between operations  14.3 us (5%)
  other arithmetic  6.63 us (2%)
    all_to_all x4, waiting for transfers between devices, send(): lax.all_to_all(buffer, 'exp', split_axis=0, concat_axis=0, tiled=True)  93.7 us
    all_to_all x4, starting transfers between devices, send(): lax.all_to_all(buffer, 'exp', split_axis=0, concat_axis=0, tiled=True)  63.8 us
    all_gather x1, waiting for transfers between devices, shards(): grads = lax.all_gather(grads, 'ctx', axis=0, tiled=False)  31.1 us
    all_gather x1, blocking collectives, shards(): hidden_all = lax.all_gather(hidden_act, 'ctx', axis=0, tiled=False)  26.5 us
    reduce_scatter x1, waiting for transfers between devices, shards(): lax.psum_scatter(gate_up, 'ctx', scatter_dimension=0, tiled=False)  11.2 us
    all_to_all x1, starting transfers between devices, shards(): back = lax.all_to_all(back, 'ctx', split_axis=0, concat_axis=0, tiled=True)  7.1 us
  transfers between devices with their start and end apart: 7, of which 5 were waited for; matrix products, arithmetic and copies ran while one was open for 11% of the time, Pallas kernels for 0%

profile of v4, /device:TPU:2, one launch (start us, length us, event | category | flops | bytes accessed | tf_op | source)
XLA Modules:
  0.0 288.5 jit_solution(1123775896365371342)
XLA Ops:
  7.2 0.9 copy.39
  9.4 1.2 convolution_convert_fusion.3
  10.6 1.4 reshape.79
  12.1 22.3 %all-to-all-start = ((bf16[64,35,128]{2,1,0:T(8,128)(2,1)}), bf16[64,35,128]{2,1,0:T(8,128)(2,1)S(1)}, u32[]{:S(2)}, u32[]{:S(2)}) async-start(bf16[64,35,128]{2,1,0:T(8,128)(2,1)} %reshape.79), calls=%async_computation | async-start | bytes 1310720 | tf_op jit(solution)/shard_map/send_tokens/all_to_all | solution.py:43
  34.9 1.4 reshape.80
  36.4 2.2 copy.49
  39.1 2.5 copy_bitcast_fusion
  41.5 31.2 %all-to-all-done = bf16[64,35,128]{2,1,0:T(8,128)(2,1)S(1)} async-done(((bf16[64,35,128]{2,1,0:T(8,128)(2,1)}), bf16[64,35,128]{2,1,0:T(8,128)(2,1)S(1)}, u32[]{:S(2)}, u32[]{:S(2)}) %all-to-all-start) | async-done | bytes 573472 | tf_op jit(solution)/shard_map/send_tokens/all_to_all | solution.py:43
  72.7 6.0 %all-to-all-start.1 = ((bf16[64,35,128]{2,1,0:T(8,128)(2,1)}), bf16[64,35,128]{2,1,0:T(8,128)(2,1)S(1)}, u32[]{:S(2)}, u32[]{:S(2)}) async-start(bf16[64,35,128]{2,1,0:T(8,128)(2,1)} %reshape.80), calls=%async_computation.1 | async-start | bytes 1310720 | tf_op jit(solution)/shard_map/send_cots/all_to_all | solution.py:43
  78.7 1.4 reshape.92
  80.2 2.7 fusion.5
  82.8 0.8 fusion.6
  83.7 1.2 pad_maximum_fusion
  84.9 31.3 %all-to-all-done.1 = bf16[64,35,128]{2,1,0:T(8,128)(2,1)S(1)} async-done(((bf16[64,35,128]{2,1,0:T(8,128)(2,1)}), bf16[64,35,128]{2,1,0:T(8,128)(2,1)S(1)}, u32[]{:S(2)}, u32[]{:S(2)}) %all-to-all-start.1) | async-done | bytes 573472 | tf_op jit(solution)/shard_map/send_cots/all_to_all | solution.py:43
  116.8 1.7 fusion.4
  118.5 7.1 %all-to-all-start.2 = ((bf16[8,320,128]{2,1,0:T(8,128)(2,1)}), bf16[8,320,128]{2,1,0:T(8,128)(2,1)S(1)}, u32[]{:S(2)}, u32[]{:S(2)}) async-start(bf16[8,320,128]{2,1,0:T(8,128)(2,1)} %fusion.4), calls=%async_computation.2 | async-start | bytes 1310720 | tf_op jit(solution)/shard_map/reduce_back/all_to_all | solution.py:80
  125.7 11.2 %reduce-scatter.2.cloned.1.call-done = bf16[1,640,128]{2,1,0:T(8,128)(2,1)} async-done(((bf16[8,640,128]{2,1,0:T(8,128)(2,1)}), bf16[1,640,128]{2,1,0:T(8,128)(2,1)}) %reduce-scatter.2.cloned.1.call-update) | async-done | bytes 163856 | tf_op jit(solution)/shard_map/reduce_gate_up/reduce_scatter | solution.py:71
  136.9 0.9 convert_element_type.111
  137.9 26.5 %all-gather = bf16[2560,128]{1,0:T(8,128)(2,1)S(1)} all-gather(bf16[320,128]{1,0:T(8,128)(2,1)S(1)} %multiply_convert_fusion.2), channel_id=2, replica_groups=mesh['ctx'=8,'exp'=64,'rep'=2] {'ctx'}, dimensions={0}, use_global_device_ids=true | all-gather | bytes 737280 | tf_op jit(solution)/shard_map/gather_hidden/all_gather | solution.py:82
  164.4 0.8 fusion.3
  165.2 1.4 reshape.83
  167.7 19.1 %all-to-all-start.3 = ((bf16[64,35,128]{2,1,0:T(8,128)(2,1)}), bf16[64,35,128]{2,1,0:T(8,128)(2,1)S(1)}, u32[]{:S(2)}, u32[]{:S(2)}) async-start(bf16[64,35,128]{2,1,0:T(8,128)(2,1)} %reshape.83), calls=%async_computation.4 | async-start | bytes 1310720 | tf_op jit(solution)/shard_map/send_out/all_to_all | solution.py:43
  186.9 31.1 %all-gather.4.cloned.1.call-done = bf16[5184,128]{1,0:T(8,128)(2,1)} async-done(((bf16[648,128]{1,0:T(8,128)(2,1)}), bf16[5184,128]{1,0:T(8,128)(2,1)}) %all-gather.4.cloned.1.call-update) | async-done | bytes 1327120 | tf_op jit(solution)/shard_map/gather_grads/all_gather | solution.py:97
  219.2 2.7 convolution_bitcast_fusion
  221.9 2.8 fusion.1
  224.7 1.7 reshape.86
  226.4 0.9 pad_maximum_fusion.1
  228.2 16.4 %all-to-all-start.4 = ((bf16[64,36,128]{2,1,0:T(8,128)(2,1)}), bf16[64,36,128]{2,1,0:T(8,128)(2,1)S(1)}, u32[]{:S(2)}, u32[]{:S(2)}) async-start(bf16[64,36,128]{2,1,0:T(8,128)(2,1)} %pad_maximum_fusion.1), calls=%async_computation.5 | async-start | bytes 1310720 | tf_op jit(solution)/shard_map/send_grad/all_to_all | solution.py:43
  244.7 1.8 reshape.84
  246.8 1.0 fusion.8
  247.8 31.2 %all-to-all-done.4 = bf16[64,36,128]{2,1,0:T(8,128)(2,1)S(1)} async-done(((bf16[64,36,128]{2,1,0:T(8,128)(2,1)}), bf16[64,36,128]{2,1,0:T(8,128)(2,1)S(1)}, u32[]{:S(2)}, u32[]{:S(2)}) %all-to-all-start.4) | async-done | bytes 589856 | tf_op jit(solution)/shard_map/send_grad/all_to_all | solution.py:43
  280.0 1.0 convolution_convert_fusion.4
  (57 shorter events, 8.0 us)
Async XLA Ops:
  7.2 109.6 %copy-start = (bf16[1,1024,896]{2,1,0:T(8,128)(2,1)S(1)}, bf16[1,1024,896]{2,1,0:T(8,128)(2,1)}, u32[]{:S(2)}) copy-start(bf16[1,1024,896]{2,1,0:T(8,128)(2,1)} %param.13) | copy-start | bytes 5505028
  8.1 26.3 %copy-start.7 = (f32[128,2]{0,1:T(2,128)S(1)}, f32[128,2]{0,1:T(2,128)}, u32[]{:S(2)}) copy-start(f32[128,2]{0,1:T(2,128)} %param.9) | copy-start | bytes 3076
  8.2 26.4 %copy-start.6 = (bf16[128,896]{1,0:T(8,128)(2,1)S(1)}, bf16[128,896]{1,0:T(8,128)(2,1)}, u32[]{:S(2)}) copy-start(bf16[128,896]{1,0:T(8,128)(2,1)} %param.10) | copy-start | bytes 688132
  12.1 60.6 %all-to-all-start = ((bf16[64,35,128]{2,1,0:T(8,128)(2,1)}), bf16[64,35,128]{2,1,0:T(8,128)(2,1)S(1)}, u32[]{:S(2)}, u32[]{:S(2)}) async-start(bf16[64,35,128]{2,1,0:T(8,128)(2,1)} %reshape.79), calls=%async_computation | async-start | bytes 1310720 | tf_op jit(solution)/shard_map/send_tokens/all_to_all | solution.py:43
  36.4 2.2 copy-start.4
  72.7 43.5 %all-to-all-start.1 = ((bf16[64,35,128]{2,1,0:T(8,128)(2,1)}), bf16[64,35,128]{2,1,0:T(8,128)(2,1)S(1)}, u32[]{:S(2)}, u32[]{:S(2)}) async-start(bf16[64,35,128]{2,1,0:T(8,128)(2,1)} %reshape.80), calls=%async_computation.1 | async-start | bytes 1310720 | tf_op jit(solution)/shard_map/send_cots/all_to_all | solution.py:43
  78.7 58.2 %reduce-scatter.2.cloned.1.call-start = ((), (), s32[]{:S(2)}) async-start(), calls=%async_computation.6 | async-start | bytes 1474560 | tf_op jit(solution)/shard_map/reduce_gate_up/reduce_scatter | solution.py:71
  80.1 2.7 copy-start.3
  80.2 2.7 copy-start.5
  118.5 48.1 %all-to-all-start.2 = ((bf16[8,320,128]{2,1,0:T(8,128)(2,1)}), bf16[8,320,128]{2,1,0:T(8,128)(2,1)S(1)}, u32[]{:S(2)}, u32[]{:S(2)}) async-start(bf16[8,320,128]{2,1,0:T(8,128)(2,1)} %fusion.4), calls=%async_computation.2 | async-start | bytes 1310720 | tf_op jit(solution)/shard_map/reduce_back/all_to_all | solution.py:80
  125.6 92.4 %all-gather.4.cloned.1.call-start = ((), (), s32[]{:S(2)}) async-start(), calls=%async_computation.7 | async-start | bytes 1492992 | tf_op jit(solution)/shard_map/gather_grads/all_gather | solution.py:97
  167.7 59.6 %all-to-all-start.3 = ((bf16[64,35,128]{2,1,0:T(8,128)(2,1)}), bf16[64,35,128]{2,1,0:T(8,128)(2,1)S(1)}, u32[]{:S(2)}, u32[]{:S(2)}) async-start(bf16[64,35,128]{2,1,0:T(8,128)(2,1)} %reshape.83), calls=%async_computation.4 | async-start | bytes 1310720 | tf_op jit(solution)/shard_map/send_out/all_to_all | solution.py:43
  219.2 2.7 copy-start.2
  227.4 0.8 copy-start.1
  228.2 50.8 %all-to-all-start.4 = ((bf16[64,36,128]{2,1,0:T(8,128)(2,1)}), bf16[64,36,128]{2,1,0:T(8,128)(2,1)S(1)}, u32[]{:S(2)}, u32[]{:S(2)}) async-start(bf16[64,36,128]{2,1,0:T(8,128)(2,1)} %pad_maximum_fusion.1), calls=%async_computation.5 | async-start | bytes 1310720 | tf_op jit(solution)/shard_map/send_grad/all_to_all | solution.py:43
Sparse Core Ops, SparseCore 0:
  85.0 51.8 reduce-scatter.1
  167.9 50.1 all-gather.3

commit v5 on v4

v5 whole, which is shorter than its diff:
```python
import jax
import jax.numpy as jnp
from jax import lax
from jax.sharding import PartitionSpec as P

LANES = 128
F32 = jnp.float32
BF16 = jnp.bfloat16


def matmul(a, b):
    return jnp.dot(a, b, preferred_element_type=F32)


def shards(tokens, routes, event_weights, cotangent, w_gate, w_up, w_down):
    owners = lax.axis_size("exp")
    parts = lax.axis_size("ctx")
    rows, fanout = routes.shape
    _, columns, hidden = w_gate.shape
    capacity = max(2, 5 * rows * fanout // (4 * owners))
    slots = owners * capacity
    piece = hidden // parts
    tiles = capacity * columns // LANES

    flat = routes.reshape(-1)
    named = (flat[:, None] == jnp.arange(owners, dtype=jnp.int32)[None, :]).astype(BF16)
    events = rows * fanout
    earlier = (
        jnp.arange(events)[:, None] > jnp.arange(events)[None, :]
    ).astype(BF16)
    before = matmul(earlier, named)
    places = jnp.sum(before * named.astype(F32), axis=1).astype(jnp.int32)
    targets = (flat * capacity + places).reshape(rows, fanout)
    slot_ids = jnp.arange(slots, dtype=jnp.int32)
    picks = [slot_ids[:, None] == targets[:, k][None, :] for k in range(fanout)]
    pick_any = sum(p.astype(BF16) for p in picks)
    slot_weights = sum(
        jnp.sum(jnp.where(p, event_weights[:, k][None, :], 0.0), axis=1)
        for k, p in enumerate(picks)
    )

    def send(buffer):
        return lax.all_to_all(buffer, "exp", split_axis=0, concat_axis=0, tiled=True)

    def spread(value):
        return lax.all_to_all(value, "ctx", split_axis=0, concat_axis=0, tiled=True)

    send_tokens = matmul(pick_any, tokens).astype(BF16)
    send_cots = (slot_weights[:, None] * matmul(pick_any, cotangent)).astype(BF16)
    received = send(
        jnp.concatenate(
            [send_tokens.reshape(owners, tiles, LANES), send_cots.reshape(owners, tiles, LANES)], axis=1
        )
    )
    gate_w = w_gate[0].reshape(columns, parts, piece).transpose(1, 0, 2)
    up_w = w_up[0].reshape(columns, parts, piece).transpose(1, 0, 2)
    received, gate_w, up_w = lax.optimization_barrier((received, gate_w, up_w))
    expert_in = received[:, :tiles].reshape(slots, columns)
    expert_cot = received[:, tiles:].reshape(slots, columns)
    down_w = w_down[0].reshape(parts, piece, columns)

    partial = jnp.concatenate(
        [
            jnp.einsum("sd,ydj->ysj", expert_in, gate_w, preferred_element_type=F32).astype(BF16),
            jnp.einsum("sd,ydj->ysj", expert_in, up_w, preferred_element_type=F32).astype(BF16),
            jnp.einsum("sd,yjd->ysj", expert_cot, down_w, preferred_element_type=F32).astype(BF16),
        ],
        axis=1,
    )
    pre = jnp.sum(spread(partial).astype(F32), axis=0)
    gate_pre, up_pre, back_pre = pre[:slots], pre[slots : 2 * slots], pre[2 * slots :]
    squash = jax.nn.sigmoid(gate_pre)
    hidden_act = (gate_pre * squash * up_pre).astype(BF16)
    grad_gate = (back_pre * up_pre * squash * (1.0 + gate_pre * (1.0 - squash))).astype(BF16)
    grad_up = (back_pre * gate_pre * squash).astype(BF16)
    inner = jnp.sum(hidden_act.astype(F32) * back_pre, axis=1)
    high = lax.reduce_precision(inner, 8, 7)
    inner_rows = jnp.stack([high, inner - high], axis=0).astype(BF16)
    inner_rows = jnp.pad(inner_rows.reshape(-1), (0, 8 * LANES - 2 * slots)).reshape(8, LANES)
    own = jnp.concatenate([hidden_act, grad_gate, grad_up, inner_rows], axis=0)
    every = spread(jnp.broadcast_to(own[None], (parts, *own.shape)))
    expert_out = jnp.einsum(
        "ysj,yjd->sd", every[:, :slots], down_w, preferred_element_type=F32
    ).astype(BF16)
    event_grad = (
        jnp.einsum("ysj,ydj->sd", every[:, slots : 2 * slots], gate_w, preferred_element_type=F32)
        + jnp.einsum("ysj,ydj->sd", every[:, 2 * slots : 3 * slots], up_w, preferred_element_type=F32)
    ).astype(BF16)
    inner = jnp.sum(every[:, 3 * slots :, :].reshape(parts, -1).astype(F32), axis=0)
    inner = inner[:slots] + inner[slots : 2 * slots]
    high = lax.reduce_precision(inner, 8, 7)
    extra = jnp.concatenate(
        [high.reshape(owners, capacity), (inner - high).reshape(owners, capacity)], axis=1
    ).astype(BF16)
    extra = jnp.pad(extra, ((0, 0), (0, LANES - 2 * capacity)))[:, None, :]
    returned = send(
        jnp.concatenate(
            [expert_out.reshape(owners, tiles, LANES), event_grad.reshape(owners, tiles, LANES), extra], axis=1
        )
    )
    back_out = returned[:, :tiles].reshape(slots, columns)
    back_grad = returned[:, tiles : 2 * tiles].reshape(slots, columns)
    extra = returned[:, 2 * tiles, : 2 * capacity].astype(F32)
    inner = (extra[:, :capacity] + extra[:, capacity:]).reshape(slots)

    mixed = sum(
        event_weights[:, k][:, None] * matmul(p.astype(BF16).T, back_out) for k, p in enumerate(picks)
    ).astype(BF16)
    token_grad = matmul(pick_any.T, back_grad).astype(BF16)
    weight_grad = (
        jnp.stack([jnp.sum(jnp.where(p, inner[:, None], 0.0), axis=0) for p in picks], axis=1)
        / event_weights
    )
    return (mixed, token_grad, weight_grad)


def solution(mesh):
    in_specs = (
        P(("rep", "exp"), "ctx"),
        P(("rep", "exp"), None),
        P(("rep", "exp"), None),
        P("exp", "ctx"),
        P("exp", "ctx", None),
        P("exp", "ctx", None),
        P("exp", None, "ctx"),
    )
    out_specs = (P(("rep", "exp"), "ctx"), P(("rep", "exp"), "ctx"), P(("rep", "exp"), None))
    return jax.shard_map(shards, mesh=mesh, in_specs=in_specs, out_specs=out_specs, check_vma=False)
```

time: 289 us -> 291 us (level)
  blocking collectives: 26.5 us -> 168 us
  waiting for transfers between devices: 136 us -> 55.5 us
  starting transfers between devices: 71 us -> 22.3 us
  between operations: 14.3 us -> 0.95 us
  local copies, waits for them, and re-layouts: 18.2 us -> 22.4 us
    all_to_all x0 -> x3, blocking collectives: none -> 168 us  [the longest x2 101 us: spread(): return lax.all_to_all(value, 'ctx', split_axis=0, concat_axis=0, tiled=True)]
    all_to_all x4 -> x1, starting transfers between devices: 63.8 us -> 22.3 us  [send(): lax.all_to_all(buffer, 'exp', split_axis=0, concat_axis=0, tiled=True)]
    all_to_all x4 -> x1, waiting for transfers between devices: 93.7 us -> 55.5 us  [send(): lax.all_to_all(buffer, 'exp', split_axis=0, concat_axis=0, tiled=True)]
    all_gather x1 -> x0, waiting for transfers between devices: 31.1 us -> none  [shards(): grads = lax.all_gather(grads, 'ctx', axis=0, tiled=False)]
    all_gather x1 -> x0, blocking collectives: 26.5 us -> none  [shards(): hidden_all = lax.all_gather(hidden_act, 'ctx', axis=0, tiled=False)]
    reduce_scatter x1 -> x0, waiting for transfers between devices: 11.2 us -> none  [shards(): lax.psum_scatter(gate_up, 'ctx', scatter_dimension=0, tiled=False)]
    all_to_all x1 -> x0, starting transfers between devices: 7.1 us -> none  [shards(): back = lax.all_to_all(back, 'ctx', split_axis=0, concat_axis=0, tiled=True)]
  transfers between devices with their start and end apart: 7 -> 1, of which waited for: 5 -> 1; matrix products, arithmetic and copies ran while one was open for 11% -> 2% of each run, Pallas kernels for 0% -> 0%
where the time goes in v5:
time: 291 us; the launch traced here: 290 us
  blocking collectives  168 us (58%)
  waiting for transfers between devices  55.5 us (19%)
  local copies, waits for them, and re-layouts  22.4 us (8%)
  starting transfers between devices  22.3 us (8%)
  matrix products  16.6 us (6%)
  other arithmetic  4.19 us (1%)
    all_to_all x2, blocking collectives, spread(): return lax.all_to_all(value, 'ctx', split_axis=0, concat_axis=0, tiled=True)  101 us
    all_to_all x1, blocking collectives, send(): lax.all_to_all(buffer, 'exp', split_axis=0, concat_axis=0, tiled=True)  67.8 us
    all_to_all x1, waiting for transfers between devices, send(): lax.all_to_all(buffer, 'exp', split_axis=0, concat_axis=0, tiled=True)  55.5 us
    all_to_all x1, starting transfers between devices, send(): lax.all_to_all(buffer, 'exp', split_axis=0, concat_axis=0, tiled=True)  22.3 us
  transfers between devices with their start and end apart: 1, of which 1 were waited for; matrix products, arithmetic and copies ran while one was open for 2% of the time, Pallas kernels for 0%

profile of v5, /device:TPU:2, one launch (start us, length us, event | category | flops | bytes accessed | tf_op | source)
XLA Modules:
  0.0 290.3 jit_solution(6280261794733080400)
XLA Ops:
  0.7 0.9 slice_bitcast_fusion
  1.5 0.8 copy.39
  2.9 0.7 multiply_add_fusion
  3.8 1.2 fusion.2
  5.0 0.6 reshape.78
  5.6 1.1 convolution_convert_fusion.3
  6.8 1.7 reshape.77
  8.5 1.3 pad_maximum_fusion.1
  9.8 22.3 %all-to-all-start = ((bf16[64,70,128]{2,1,0:T(8,128)(2,1)}), bf16[64,70,128]{2,1,0:T(8,128)(2,1)S(1)}, u32[]{:S(2)}, u32[]{:S(2)}) async-start(bf16[64,70,128]{2,1,0:T(8,128)(2,1)} %pad_maximum_fusion.1), calls=%async_computation | async-start | bytes 2359296 | tf_op jit(solution)/shard_map/all_to_all | solution.py:43
  32.1 2.2 copy.49
  34.8 2.5 copy_bitcast_fusion
  37.4 55.5 %all-to-all-done = bf16[64,70,128]{2,1,0:T(8,128)(2,1)S(1)} async-done(((bf16[64,70,128]{2,1,0:T(8,128)(2,1)}), bf16[64,70,128]{2,1,0:T(8,128)(2,1)S(1)}, u32[]{:S(2)}, u32[]{:S(2)}) %all-to-all-start) | async-done | bytes 1146912 | tf_op jit(solution)/shard_map/all_to_all | solution.py:43
  92.9 1.3 fusion.36
  94.1 1.7 reshape.87
  95.9 1.8 reshape.88
  97.7 2.5 fusion.5
  100.2 0.8 fusion.6
  101.0 0.9 fusion.4
  102.0 52.5 %all_to_all.20 = bf16[8,960,128]{2,1,0:T(8,128)(2,1)S(1)} all-to-all(bf16[8,960,128]{2,1,0:T(8,128)(2,1)S(1)} %pad_maximum_fusion), channel_id=1, replica_groups=mesh['ctx'=8,'exp'=64,'rep'=2] {'ctx'}, dimensions={0} | all-to-all | bytes 3932160 | tf_op jit(solution)/shard_map/all_to_all | solution.py:46
  155.5 48.1 %all_to_all.21 = bf16[8,968,128]{2,1,0:T(8,128)(2,1)S(1)} all-to-all(bf16[8,968,128]{2,1,0:T(8,128)(2,1)S(1)} %broadcast_in_dim.55), channel_id=1, replica_groups=mesh['ctx'=8,'exp'=64,'rep'=2] {'ctx'}, dimensions={0} | all-to-all | bytes 3964928 | tf_op jit(solution)/shard_map/all_to_all | solution.py:46
  203.5 1.3 copy-done.2
  205.3 1.9 fusion.3
  207.2 0.6 reshape.82
  207.8 2.7 convolution_bitcast_fusion
  210.5 2.8 fusion.1
  213.3 1.7 reshape.83
  215.4 67.8 %all_to_all.22 = bf16[64,71,128]{2,1,0:T(8,128)(2,1)S(1)} all-to-all(bf16[64,71,128]{2,1,0:T(8,128)(2,1)S(1)} %pad_maximum_fusion.2), channel_id=1, replica_groups=mesh['ctx'=8,'exp'=64,'rep'=2] {'exp'}, dimensions={0} | all-to-all | bytes 2326528 | tf_op jit(solution)/shard_map/all_to_all | solution.py:43
  283.6 1.3 fusion.35
  284.9 1.8 reshape.85
  286.7 1.0 convolution_convert_fusion.4
  287.8 0.6 reshape.84
  288.7 1.0 fusion.8
  (47 shorter events, 4.4 us)
Async XLA Ops:
  0.6 100.4 %copy-start = (bf16[1,1024,896]{2,1,0:T(8,128)(2,1)S(1)}, bf16[1,1024,896]{2,1,0:T(8,128)(2,1)}, u32[]{:S(2)}) copy-start(bf16[1,1024,896]{2,1,0:T(8,128)(2,1)} %param.13) | copy-start | bytes 5505028
  0.6 5.0 %copy-start.6 = (bf16[128,896]{1,0:T(8,128)(2,1)S(1)}, bf16[128,896]{1,0:T(8,128)(2,1)}, u32[]{:S(2)}) copy-start(bf16[128,896]{1,0:T(8,128)(2,1)} %param.7) | copy-start | bytes 688132
  9.8 83.1 %all-to-all-start = ((bf16[64,70,128]{2,1,0:T(8,128)(2,1)}), bf16[64,70,128]{2,1,0:T(8,128)(2,1)S(1)}, u32[]{:S(2)}, u32[]{:S(2)}) async-start(bf16[64,70,128]{2,1,0:T(8,128)(2,1)} %pad_maximum_fusion.1), calls=%async_computation | async-start | bytes 2359296 | tf_op jit(solution)/shard_map/all_to_all | solution.py:43
  32.1 2.2 copy-start.5
  97.7 2.5 copy-start.4
  203.5 1.3 copy-start.2
  207.8 2.7 copy-start.3
  284.9 2.8 copy-start.1
  287.8 2.0 copy-start.7
